TPU v7x, 32 devices: a whole 2x2x4 slice. The times are simulated.
32 devices in a mesh: groups: 2 (over y), dp: 16 (over z, x, core).
Axes of the slice: x: 2, y: 2, z: 4, core: 2. Of those that a mesh axis runs over, the one named last changes fastest.
Arguments:
- particles: bfloat16 [2048, 128, 128], P(('groups', 'dp')), parts along dimension 0, may hold values from -20 to 20
- refs: bfloat16 [128, 256, 128], P('dp', 'groups'), parts along dimension 1, may hold values from -0.5 to 0.5
- ctf_group: int32 [2048], P(('groups', 'dp')), parts along dimension 0, may hold values from 0 to 31, as said below
- defocus: float32 [64], P('groups'), parts along dimension 0, may hold values from 0.5 to 2
- class_prior: float32 [256], P('groups'), parts along dimension 0, may hold values from 0.25 to 4
- cycle_weight: float32 [64], replicated, may hold values from 0.5 to 2
Outputs:
- new_refs: float32 [128, 256, 128], P('dp', 'groups'), parts along dimension 1
- log_evidence: float32 [2048], P(('groups', 'dp')), parts along dimension 0
There are 2 independent parts, one for each index of `groups`. A program takes and returns all parts, laid end to end along the dimension named above; an argument that names none is the same for every part. Nothing has to cross between parts.
Inputs may be any that keep to these rules, and one draw needn't show every extreme that they name: `ctf_group`: CTF groups follow the particle order: particle n belongs to group n * 32 // 1024 or the next one, capped at 31.
All inputs are finite; a program needn't handle non-finite values.
Results may differ from a plain program's by a relative error of at most 0.0045.
Values may be sent and summed in bfloat16 or wider, within the bound.
A program may use at most 64 MiB of HBM per device.

v0:
```python
import functools
import math

import jax
import jax.numpy as jnp
from jax import lax
from jax.experimental import pallas as pl
from jax.experimental.pallas import tpu as pltpu
from jax.sharding import PartitionSpec as P

R = 64
ROT = 36
HALF = ROT // 2
NC = HALF + 1
G = 32
MESH = pl.DeviceIdType.MESH
HIGHEST = lax.Precision.HIGHEST


def dev(index):
    return {"dp": index}


def ring_steps(zn):
    plus = zn // 2
    minus = zn - 1 - plus
    steps = []
    for d in range(1, plus + 1):
        steps.append((1, d))
        if d <= minus:
            steps.append((-1, d))
    return steps


def gather_kernel(zn, dp, window, refs_ref, part_ref, row_ref, focus_ref, cw_ref, prior_ref,
                  wt_ref, wpart_ref, table_ref, pp_ref, ev_ref, mass_ref,
                  out_ref, cres, energy, bias, psum, evcol, local_sem, send, recv, wsend, wrecv):
    me = lax.axis_index("dp")
    z, x, c = me // 4, (me // 2) % 2, me % 2
    flip_x = z * 4 + (1 - x) * 2 + c
    flip_c = z * 4 + x * 2 + (1 - c)
    n, m_all, q = part_ref.shape
    mb, k, _ = refs_ref.shape
    nall = n * dp
    steps = [(s, d) for d in range(1, zn) for s in (1, -1)]
    beside = {s: lax.rem(z + zn + s, zn) * 4 + x * 2 + c for s in (1, -1)}

    def holds(s, d):
        return z >= d if s == 1 else z + d < zn

    def goes(s):
        return z + 1 < zn if s == 1 else z >= 1

    def origin(s, d):
        return lax.rem(z + zn - s * d, zn) * 4

    barrier = pltpu.get_barrier_semaphore()
    greet = [beside[1], beside[-1], flip_x, flip_c]
    for p in greet:
        pl.semaphore_signal(barrier, inc=1, device_id=dev(p), device_id_type=MESH)
    pl.semaphore_wait(barrier, len(greet))

    count = 2 * (zn - 1)
    x0, c0 = count, 2 * count + 1

    def copy_of(src, block, target, slot):
        return pltpu.make_async_remote_copy(
            src_ref=src,
            dst_ref=out_ref.at[block],
            send_sem=send.at[slot],
            recv_sem=recv.at[slot],
            device_id=dev(target),
            device_id_type=MESH,
        )

    slot_of = {step: i for i, step in enumerate(steps)}
    for s in (1, -1):
        @pl.when(goes(s))
        def _():
            copy_of(refs_ref, me, beside[s], slot_of[(s, 1)]).start()
    copy_of(refs_ref, me, flip_x, x0).start()
    copy_of(refs_ref, me, flip_c, c0).start()
    keep = pltpu.make_async_copy(refs_ref, out_ref.at[me], local_sem)
    keep.start()

    lane = lax.broadcasted_iota(jnp.int32, (G, q), 1)
    radius = (jnp.where(lane < R, lane, lane - R).astype(jnp.float32) + 1.0) / R
    eye = lax.broadcasted_iota(jnp.int32, (G, G), 0) == lax.broadcasted_iota(jnp.int32, (G, G), 1)
    focus = jnp.sum(jnp.where(eye, jnp.broadcast_to(focus_ref[...], (G, G)), 0.0), axis=1, keepdims=True)
    phase = 20.0 * focus * (radius * radius)
    ctf = -(0.995 * jnp.sin(phase) + 0.1 * jnp.cos(phase))
    cw = jnp.concatenate([cw_ref[...], cw_ref[...]], axis=1)
    gain_table = cw * ctf
    power = gain_table * ctf

    def dot(a, b):
        return jnp.dot(a, b, precision=HIGHEST, preferred_element_type=jnp.float32)

    onehot = (row_ref[...] == lax.broadcasted_iota(jnp.int32, (G, n), 0)).astype(jnp.float32)

    def picked(table):
        return lax.dot_general(
            onehot, table, (((0,), (0,)), ((), ())),
            preferred_element_type=jnp.float32, precision=HIGHEST,
        )

    gain = picked(gain_table)
    anorm = 0.5 * picked(power)
    start = (me * (n * G)) // nall
    hot = (
        row_ref[...] == lax.broadcasted_iota(jnp.int32, (window, n), 0) + start
    ).astype(jnp.float32)
    below = lax.broadcasted_iota(jnp.int32, (window, G), 0) - lax.broadcasted_iota(jnp.int32, (window, G), 1)
    for d in range(dp):
        pick = (below == -(d * n * G // nall)).astype(jnp.float32)
        table_ref[d * window:(d + 1) * window, :] = dot(pick, power)

    chunk = 16

    @pl.loop(0, m_all // chunk)
    def _(i):
        at = pl.ds(pl.multiple_of(i * chunk, chunk), chunk)
        wide = part_ref[:, at, :].astype(jnp.float32) * gain[:, None, :]
        wt_ref[at] = jnp.swapaxes(wide, 0, 1).astype(jnp.bfloat16)

    wcopies = []
    for b in range(dp // 2):
        copy = pltpu.make_async_remote_copy(
            src_ref=wt_ref.at[pl.ds((2 * b + 1 - c) * mb, mb)],
            dst_ref=wpart_ref.at[b],
            send_sem=wsend.at[b],
            recv_sem=wrecv.at[b],
            device_id=dev(flip_c),
            device_id_type=MESH,
        )
        copy.start()
        wcopies.append(copy)

    cres[...] = jnp.zeros_like(cres)
    energy[...] = jnp.zeros_like(energy)
    lane_n = lax.broadcasted_iota(jnp.int32, (n, q), 1)
    sign = jnp.where(lane_n < R, jnp.float32(1.0), jnp.float32(-1.0))

    def products(block):
        @pl.loop(0, mb)
        def _(i):
            m = block * mb + i
            r = lax.rem(m, ROT)
            w = wt_ref[m]
            turned = (pltpu.roll(w.astype(jnp.float32), R, 1) * sign).astype(jnp.bfloat16)
            both = jnp.concatenate([w, turned], axis=0)
            ref = out_ref[block, i]
            cres[r] += lax.dot_general(
                both, ref, (((1,), (1,)), ((), ())), preferred_element_type=jnp.float32
            )
            wide = ref.astype(jnp.float32)
            energy[...] += wide * wide

    keep.wait()
    products(me)
    for i, (s, d) in enumerate(steps):
        @pl.when(holds(s, d))
        def _():
            block = origin(s, d) + x * 2 + c
            copy_of(out_ref.at[block], block, beside[s], slot_of[(s, d)]).wait_recv()
            if d + 1 < zn:
                @pl.when(goes(s))
                def _():
                    copy_of(out_ref.at[block], block, beside[s], slot_of[(s, d + 1)]).start()
            copy_of(out_ref.at[block], block, flip_x, x0 + 1 + i).start()
            copy_of(out_ref.at[block], block, flip_c, c0 + 1 + i).start()
            products(block)
    every = [(None, (1, 0))] + list(enumerate(steps))

    def guarded(s, d, body):
        if d == 0:
            body()
        else:
            pl.when(holds(s, d))(body)

    for i, (s, d) in every:
        j = 0 if i is None else i + 1

        def from_x(s=s, d=d, j=j):
            block = origin(s, d) + (1 - x) * 2 + c
            copy_of(out_ref.at[block], block, flip_x, x0 + j).wait_recv()
            copy_of(out_ref.at[block], block, flip_c, c0 + count + 1 + j).start()
            products(block)
            mine = origin(s, d) + x * 2 + (1 - c)
            copy_of(out_ref.at[mine], mine, flip_c, c0 + j).wait_recv()
            products(mine)

        guarded(s, d, from_x)
    for i, (s, d) in every:
        j = 0 if i is None else i + 1

        def from_core(s=s, d=d, j=j):
            block = origin(s, d) + (1 - x) * 2 + (1 - c)
            copy_of(out_ref.at[block], block, flip_c, c0 + count + 1 + j).wait_recv()
            products(block)

        guarded(s, d, from_core)

    scores_and_posterior(anorm, hot, prior_ref, pp_ref, ev_ref, mass_ref, cres, energy, bias, psum, evcol, n)

    for copy in wcopies:
        copy.wait()
    for i, (s, d) in every:
        j = 0 if i is None else i + 1

        def sent(s=s, d=d, j=j):
            block = origin(s, d) + x * 2 + c
            other = origin(s, d) + (1 - x) * 2 + c
            copy_of(out_ref.at[block], block, flip_x, x0 + j).wait_send()
            copy_of(out_ref.at[block], block, flip_c, c0 + j).wait_send()
            copy_of(out_ref.at[other], other, flip_c, c0 + count + 1 + j).wait_send()

        guarded(s, d, sent)
    for s in (1, -1):
        for d in range(0, zn - 1):
            room = jnp.minimum(z - d, zn - 2 - z) if s == 1 else jnp.minimum(zn - 1 - d - z, z - 1)

            @pl.when(room >= 0)
            def _():
                block = origin(s, d) + x * 2 + c
                copy_of(out_ref.at[block], block, beside[s], slot_of[(s, d + 1)]).wait_send()


def dft_even_odd(even_in, odd_in, use_cos):
    f = math.cos if use_cos else math.sin

    def one(items, j):
        total = None
        for i, v in items:
            w = f(2.0 * math.pi * ((i * j) % ROT) / ROT)
            if abs(w) < 1e-12:
                continue
            if abs(w - 1.0) < 1e-12:
                term = v
            elif abs(w + 1.0) < 1e-12:
                term = -v
            else:
                term = v * jnp.float32(w)
            total = term if total is None else total + term
        return total

    count = HALF // 2 + 1
    return [one(even_in, j) for j in range(count)], [one(odd_in, j) for j in range(count)]


def half_transform(values, use_cos):
    even = [(i, v) for i, v in values.items() if i % 2 == 0]
    odd = [(i, v) for i, v in values.items() if i % 2 == 1]
    es, os_ = dft_even_odd(even, odd, use_cos)
    zero = jnp.zeros_like(next(iter(values.values())))
    out = {}
    for j in range(HALF // 2 + 1):
        e = zero if es[j] is None else es[j]
        o = zero if os_[j] is None else os_[j]
        out[j] = e + o
        out[HALF - j] = (e - o) if use_cos else (o - e)
    return out


def scores_and_posterior(anorm, hot, prior_ref, pp_ref, ev_ref, mass_ref, cres, energy, bias, psum, evcol, n):
    norm = lax.dot_general(
        anorm, energy[...], (((1,), (1,)), ((), ())),
        preferred_element_type=jnp.float32, precision=HIGHEST,
    )
    bias[...] = jnp.log(prior_ref[...]) - norm

    rows = 16

    @pl.loop(0, n // rows)
    def _(i):
        at = pl.ds(pl.multiple_of(i * rows, rows), rows)
        at_im = pl.ds(pl.multiple_of(n + i * rows, rows), rows)
        a = {0: cres[0, at, :], HALF: cres[HALF, at, :]}
        b = {}
        for r in range(1, HALF):
            a[r] = cres[r, at, :] + cres[ROT - r, at, :]
            b[r] = cres[r, at_im, :] - cres[ROT - r, at_im, :]
        cosine = half_transform(a, True)
        sine = half_transform(b, False)
        add = bias[at, :]
        scores = {}
        for j in range(NC):
            base = cosine[j] + add
            if j in (0, HALF):
                scores[j] = base
            else:
                scores[j] = base - sine[j]
                scores[ROT - j] = base + sine[j]
        top = scores[0]
        for j in range(1, ROT):
            top = jnp.maximum(top, scores[j])
        top = jnp.max(top, axis=1, keepdims=True)
        total = None
        expo = {}
        for j in range(ROT):
            expo[j] = jnp.exp(scores[j] - top)
            total = expo[j] if total is None else total + expo[j]
        norm_total = jnp.sum(total, axis=1, keepdims=True)
        evcol[at, :] = jnp.broadcast_to(top + jnp.log(norm_total), (rows, n))
        inv = 1.0 / norm_total
        psum[at, :] = total * inv
        u = {0: expo[0] * inv, HALF: expo[HALF] * inv}
        v = {}
        for j in range(1, HALF):
            u[j] = (expo[j] + expo[ROT - j]) * inv
            v[j] = (expo[j] - expo[ROT - j]) * inv
        real = half_transform(u, True)
        imag = half_transform(v, False)
        for r in range(NC):
            pp_ref[r, at, :] = real[r].astype(jnp.bfloat16)
            pp_ref[NC + r, at, :] = imag[r].astype(jnp.bfloat16)

    square = (n, n)
    eye = lax.broadcasted_iota(jnp.int32, square, 0) == lax.broadcasted_iota(jnp.int32, square, 1)
    ev_ref[...] = jnp.sum(jnp.where(eye, evcol[...], 0.0), axis=0, keepdims=True)
    mass_ref[...] = lax.dot_general(
        hot, psum[...], (((1,), (0,)), ((), ())),
        preferred_element_type=jnp.float32, precision=HIGHEST,
    )


def mstep_kernel(zn, dp, pp_ref, wt_ref, wpart_ref, mass_ref, table_ref, out_ref,
                 pbuf, pt, xsend, xrecv, acc, zsend, zrecv, mslots,
                 psend_s, psend_r, xs, xr, zs, zr, ms, mr):
    me = lax.axis_index("dp")
    z, x, c = me // 4, (me // 2) % 2, me % 2
    flip_x = z * 4 + (1 - x) * 2 + c
    flip_c = z * 4 + x * 2 + (1 - c)
    mb, k, q = out_ref.shape

    barrier = pltpu.get_barrier_semaphore()
    for o in range(1, dp):
        pl.semaphore_signal(barrier, inc=1, device_id=dev(lax.rem(me + o, dp)), device_id_type=MESH)
    pl.semaphore_wait(barrier, dp - 1)

    pcopy = pltpu.make_async_remote_copy(
        src_ref=pp_ref, dst_ref=pbuf, send_sem=psend_s, recv_sem=psend_r,
        device_id=dev(flip_c), device_id_type=MESH,
    )
    pcopy.start()
    mcopies = []
    for o in range(1, dp):
        copy = pltpu.make_async_remote_copy(
            src_ref=mass_ref, dst_ref=mslots.at[me], send_sem=ms.at[o], recv_sem=mr.at[o],
            device_id=dev(lax.rem(me + o, dp)), device_id_type=MESH,
        )
        copy.start()
        mcopies.append(copy)
    mslots[me] = mass_ref[...]
    pcopy.wait()

    @pl.loop(0, 2 * NC)
    def _(i):
        pt[i] = jnp.concatenate([pp_ref[i], pbuf[i]], axis=0).T

    lane = lax.broadcasted_iota(jnp.int32, (k, q), 1)
    mask = jnp.where(lane < R, jnp.float32(-1.0), jnp.float32(1.0))

    def numer(zx, i):
        m = (zx * 2 + c) * mb + i
        r = lax.rem(m, ROT)
        rr = jnp.minimum(r, ROT - r)
        s = jnp.where(r > HALF, -1, 1).astype(jnp.float32)
        w = jnp.concatenate([wt_ref[m], wpart_ref[zx, i]], axis=0)
        u = jnp.dot(pt[rr], w, preferred_element_type=jnp.float32)
        v = jnp.dot(pt[NC + rr], w, preferred_element_type=jnp.float32)
        return u + pltpu.roll(v, R, 1) * (mask * s)

    steps = ring_steps(zn)
    reach = {1: zn // 2, -1: zn - 1 - zn // 2}
    order = [((s * (reach[s] + 1 - d)) % zn, s, d) for s, d in steps] + [(0, 0, 0)]
    xcopies = []
    for o, _, _ in order:
        zz = lax.rem(z + o, zn)

        @pl.loop(0, mb)
        def _(i):
            xsend[o, i] = numer(zz * 2 + 1 - x, i).astype(jnp.bfloat16)

        copy = pltpu.make_async_remote_copy(
            src_ref=xsend.at[o], dst_ref=xrecv.at[o], send_sem=xs.at[o], recv_sem=xr.at[o],
            device_id=dev(flip_x), device_id_type=MESH,
        )
        copy.start()
        xcopies.append(copy)

    zcopies = {}
    last = []
    for j, ((o, s, d), xcopy) in enumerate(zip(order, xcopies)):
        zz = lax.rem(z + o, zn)

        @pl.loop(0, mb)
        def _(i):
            acc[i] = numer(zz * 2 + x, i)

        xcopy.wait_recv()
        if o:
            before = None
            if d > 1:
                before, got = zcopies[(s, d - 1)]
                got.wait_recv()

            @pl.loop(0, mb)
            def _(i):
                total = acc[i] + xrecv[o, i].astype(jnp.float32)
                if before is not None:
                    total = total + zrecv[before, i].astype(jnp.float32)
                zsend[j, i] = total.astype(jnp.bfloat16)

            copy = pltpu.make_async_remote_copy(
                src_ref=zsend.at[j], dst_ref=zrecv.at[j], send_sem=zs.at[j], recv_sem=zr.at[j],
                device_id=dev(lax.rem(z + zn + s, zn) * 4 + x * 2 + c), device_id_type=MESH,
            )
            copy.start()
            zcopies[(s, d)] = (j, copy)
            if d == reach[s]:
                last.append((j, copy))
    for copy in mcopies:
        copy.wait_recv()
    wide = mslots[...].reshape(dp * mslots.shape[1], k)
    denom = 1.0 + lax.dot_general(
        wide, table_ref[...], (((0,), (0,)), ((), ())),
        preferred_element_type=jnp.float32, precision=HIGHEST,
    )
    inv = 1.0 / denom
    for _, copy in last:
        copy.wait_recv()

    @pl.loop(0, mb)
    def _(i):
        total = acc[i] + xrecv[0, i].astype(jnp.float32)
        for j, _ in last:
            total = total + zrecv[j, i].astype(jnp.float32)
        out_ref[i] = total * inv

    for copy in xcopies + [copy for _, copy in zcopies.values()] + mcopies:
        copy.wait_send()


def shards(dp, particles, refs, ctf_group, defocus, class_prior, cycle_weight):
    n, m_all, q = particles.shape
    mb, k, _ = refs.shape
    zn = dp // 4
    nall = n * dp
    window = -(-((n * G) // nall + 2) // 8) * 8

    vmem = pl.BlockSpec(memory_space=pltpu.VMEM)
    hbm = pl.BlockSpec(memory_space=pl.ANY)
    sem = pltpu.SemaphoreType.DMA
    copies = 8 * zn - 5
    wt, wpart, table, pp, ev, mass = pl.pallas_call(
        functools.partial(gather_kernel, zn, dp, window),
        out_shape=(
            jax.ShapeDtypeStruct((m_all, n, q), jnp.bfloat16),
            jax.ShapeDtypeStruct((dp // 2, mb, n, q), jnp.bfloat16),
            jax.ShapeDtypeStruct((dp * window, q), jnp.float32),
            jax.ShapeDtypeStruct((2 * NC, n, k), jnp.bfloat16),
            jax.ShapeDtypeStruct((1, n), jnp.float32),
            jax.ShapeDtypeStruct((window, k), jnp.float32),
        ),
        in_specs=[vmem] * 6,
        out_specs=(vmem, hbm, vmem, vmem, vmem, vmem),
        scratch_shapes=[
            pltpu.VMEM((dp, mb, k, q), jnp.bfloat16),
            pltpu.VMEM((ROT, 2 * n, k), jnp.float32),
            pltpu.VMEM((k, q), jnp.float32),
            pltpu.VMEM((n, k), jnp.float32),
            pltpu.VMEM((n, k), jnp.float32),
            pltpu.VMEM((n, n), jnp.float32),
            sem, sem((copies,)), sem((copies,)), sem((dp // 2,)), sem((dp // 2,)),
        ],
        compiler_params=pltpu.CompilerParams(collective_id=0, has_side_effects=True),
        name="gather",
    )(refs, particles, ctf_group[None, :], defocus[None, :], cycle_weight[None, :], class_prior[None, :])

    new_refs = pl.pallas_call(
        functools.partial(mstep_kernel, zn, dp),
        out_shape=jax.ShapeDtypeStruct((mb, k, q), jnp.float32),
        in_specs=[vmem] * 5,
        out_specs=vmem,
        scratch_shapes=[
            pltpu.VMEM((2 * NC, n, k), jnp.bfloat16),
            pltpu.VMEM((2 * NC, k, 2 * n), jnp.bfloat16),
            pltpu.VMEM((zn, mb, k, q), jnp.bfloat16),
            pltpu.VMEM((zn, mb, k, q), jnp.bfloat16),
            pltpu.VMEM((mb, k, q), jnp.float32),
            pltpu.VMEM((zn, mb, k, q), jnp.bfloat16),
            pltpu.VMEM((zn, mb, k, q), jnp.bfloat16),
            pltpu.VMEM((dp, window, k), jnp.float32),
            sem, sem,
            sem((zn,)), sem((zn,)), sem((zn,)), sem((zn,)), sem((dp,)), sem((dp,)),
        ],
        compiler_params=pltpu.CompilerParams(collective_id=1, has_side_effects=True),
        name="mstep",
    )(pp, wt, wpart, mass, table)
    return (new_refs, ev[0])


def solution(mesh):
    in_specs = (
        P(("groups", "dp"), None, None),
        P("dp", "groups", None),
        P(("groups", "dp")),
        P("groups"),
        P("groups"),
        P(),
    )
    out_specs = (P("dp", "groups", None), P(("groups", "dp")))
    return jax.shard_map(
        functools.partial(shards, mesh.shape["dp"]),
        mesh=mesh, in_specs=in_specs, out_specs=out_specs, check_vma=False,
    )
```

profile of v0, /device:TPU:0, one launch (start us, length us, event | category | flops | bytes accessed | tf_op | source)
XLA Modules:
  0.0 95.6 jit_solution(4617481235125399897)
XLA Ops:
  0.6 52.9 %gather.1 = (bf16[128,64,128]{2,1,0:T(8,128)(2,1)}, bf16[8,8,64,128]{3,2,1,0:T(8,128)(2,1)}, f32[128,128]{1,0:T(8,128)}, bf16[38,64,128]{2,1,0:T(8,128)(2,1)}, f32[1,64]{1,0:T(1,128)}, /*index=5*/f32[8,128]{1,0:T(8,128)}) custom-call(bf16[8,128,128]{2,1,0:T(8,128)(2,1)} %refs_ref.1, bf16[64,128,128]{2,1,0:T(8,128)(2,1)} %part_ref.1, s32[1,64]{1,0:T(1,128)} %bitcast.5, ...), custom_call_target="tpu_custom_call" | custom-call | tf_op jit(solution)/shard_map/gather/pallas_call | solution.py:456
  53.6 0.0 copy-start
  53.6 39.7 %mstep.1 = f32[8,128,128]{2,1,0:T(8,128)} custom-call(bf16[38,64,128]{2,1,0:T(8,128)(2,1)} %get-tuple-element.8.pp_ref, bf16[128,64,128]{2,1,0:T(8,128)(2,1)} %get-tuple-element.9.wt_ref, bf16[8,8,64,128]{3,2,1,0:T(8,128)(2,1)} %get-tuple-element.10.wpart_ref, f32[8,128]{1,0:T(8,128)} %get-tuple-element.11.mass_ref, f32[128,128]{1,0:T(8,128)} %get-tuple-element.12.table_ref), custom_call_target="tpu_custom_call" | custom-call | tf_op jit(solution)/shard_map/mstep/pallas_call | solution.py:481
  93.2 1.9 %copy.10 = f32[8,128,128]{2,1,0:T(8,128)} copy(f32[8,128,128]{2,1,0:T(8,128)} %mstep.1) | data formatting | bytes 1048576
  95.1 0.0 copy-done
  95.1 0.5 copy.11
Async XLA Ops:
  53.6 41.6 %copy-start = (f32[1,64]{1,0:T(1,128)S(1)}, f32[1,64]{1,0:T(1,128)}, u32[]{:S(2)}) copy-start(f32[1,64]{1,0:T(1,128)} %get-tuple-element.13) | copy-start | bytes 772
where the time goes:
time: 95.8 us; the launch traced here: 95.6 us
  Pallas kernels  92.6 us (97%)
  local copies, waits for them, and re-layouts  2.39 us (2%)
    pallas_call x1, Pallas kernels, shards(): pl.pallas_call(functools.partial(gather_kernel, zn, dp, window), out_shap...  52.9 us
    pallas_call x1, Pallas kernels, shards(): pl.pallas_call(functools.partial(mstep_kernel, zn, dp), out_shape=jax.Sha...  39.7 us
    unnamed x4, local copies, waits for them, and re-layouts  2.39 us

commit v1 on v0

--- a/solution.py
+++ b/solution.py
@@ -142,8 +142,8 @@
     sign = jnp.where(lane_n < R, jnp.float32(1.0), jnp.float32(-1.0))
 
     def products(block):
-        @pl.loop(0, mb)
-        def _(i):
+        total = None
+        for i in range(mb):
             m = block * mb + i
             r = lax.rem(m, ROT)
             w = wt_ref[m]
@@ -154,7 +154,8 @@
                 both, ref, (((1,), (1,)), ((), ())), preferred_element_type=jnp.float32
             )
             wide = ref.astype(jnp.float32)
-            energy[...] += wide * wide
+            total = wide * wide if total is None else total + wide * wide
+        energy[...] += total
 
     keep.wait()
     products(me)
@@ -378,8 +379,7 @@
     for o, _, _ in order:
         zz = lax.rem(z + o, zn)
 
-        @pl.loop(0, mb)
-        def _(i):
+        for i in range(mb):
             xsend[o, i] = numer(zz * 2 + 1 - x, i).astype(jnp.bfloat16)
 
         copy = pltpu.make_async_remote_copy(
@@ -394,8 +394,7 @@
     for j, ((o, s, d), xcopy) in enumerate(zip(order, xcopies)):
         zz = lax.rem(z + o, zn)
 
-        @pl.loop(0, mb)
-        def _(i):
+        for i in range(mb):
             acc[i] = numer(zz * 2 + x, i)
 
         xcopy.wait_recv()

time: 95.8 us -> 80.7 us (0.84)
  Pallas kernels: 92.6 us -> 77.5 us
    pallas_call x1, Pallas kernels: 52.9 us -> 39.5 us  [shards(): pl.pallas_call(functools.partial(gather_kernel, zn, dp, window), out_shap...]
    pallas_call x1, Pallas kernels: 39.7 us -> 37.9 us  [shards(): pl.pallas_call(functools.partial(mstep_kernel, zn, dp), out_shape=jax.Sha...]
where the time goes in v1:
time: 80.7 us; the launch traced here: 80.5 us
  Pallas kernels  77.5 us (96%)
  local copies, waits for them, and re-layouts  2.39 us (3%)
    pallas_call x1, Pallas kernels, shards(): pl.pallas_call(functools.partial(gather_kernel, zn, dp, window), out_shap...  39.5 us
    pallas_call x1, Pallas kernels, shards(): pl.pallas_call(functools.partial(mstep_kernel, zn, dp), out_shape=jax.Sha...  37.9 us
    unnamed x4, local copies, waits for them, and re-layouts  2.39 us

profile of v1, /device:TPU:0, one launch (start us, length us, event | category | flops | bytes accessed | tf_op | source)
XLA Modules:
  0.0 80.5 jit_solution(6036149742231461478)
XLA Ops:
  0.6 39.5 %gather.1 = (bf16[128,64,128]{2,1,0:T(8,128)(2,1)}, bf16[8,8,64,128]{3,2,1,0:T(8,128)(2,1)}, f32[128,128]{1,0:T(8,128)}, bf16[38,64,128]{2,1,0:T(8,128)(2,1)}, f32[1,64]{1,0:T(1,128)}, /*index=5*/f32[8,128]{1,0:T(8,128)}) custom-call(bf16[8,128,128]{2,1,0:T(8,128)(2,1)} %refs_ref.1, bf16[64,128,128]{2,1,0:T(8,128)(2,1)} %part_ref.1, s32[1,64]{1,0:T(1,128)} %bitcast.5, ...), custom_call_target="tpu_custom_call" | custom-call | tf_op jit(solution)/shard_map/gather/pallas_call | solution.py:455
  40.2 0.0 copy-start
  40.2 37.9 %mstep.1 = f32[8,128,128]{2,1,0:T(8,128)} custom-call(bf16[38,64,128]{2,1,0:T(8,128)(2,1)} %get-tuple-element.8.pp_ref, bf16[128,64,128]{2,1,0:T(8,128)(2,1)} %get-tuple-element.9.wt_ref, bf16[8,8,64,128]{3,2,1,0:T(8,128)(2,1)} %get-tuple-element.10.wpart_ref, f32[8,128]{1,0:T(8,128)} %get-tuple-element.11.mass_ref, f32[128,128]{1,0:T(8,128)} %get-tuple-element.12.table_ref), custom_call_target="tpu_custom_call" | custom-call | tf_op jit(solution)/shard_map/mstep/pallas_call | solution.py:480
  78.1 1.9 %copy.10 = f32[8,128,128]{2,1,0:T(8,128)} copy(f32[8,128,128]{2,1,0:T(8,128)} %mstep.1) | data formatting | bytes 1048576
  80.0 0.0 copy-done
  80.0 0.5 copy.11
Async XLA Ops:
  40.2 39.8 %copy-start = (f32[1,64]{1,0:T(1,128)S(1)}, f32[1,64]{1,0:T(1,128)}, u32[]{:S(2)}) copy-start(f32[1,64]{1,0:T(1,128)} %get-tuple-element.13) | copy-start | bytes 772

commit v2 on v1

v2 whole, which is shorter than its diff:
```python
import functools
import math

import jax
import jax.numpy as jnp
from jax import lax
from jax.experimental import pallas as pl
from jax.experimental.pallas import tpu as pltpu
from jax.sharding import PartitionSpec as P

R = 64
ROT = 36
HALF = ROT // 2
NC = HALF + 1
G = 32
MESH = pl.DeviceIdType.MESH
HIGHEST = lax.Precision.HIGHEST
F32 = jnp.float32
BF16 = jnp.bfloat16


def dev(index):
    return {"dp": index}


def dft_even_odd(even_in, odd_in, use_cos):
    f = math.cos if use_cos else math.sin

    def one(items, j):
        total = None
        for i, v in items:
            w = f(2.0 * math.pi * ((i * j) % ROT) / ROT)
            if abs(w) < 1e-12:
                continue
            if abs(w - 1.0) < 1e-12:
                term = v
            elif abs(w + 1.0) < 1e-12:
                term = -v
            else:
                term = v * jnp.float32(w)
            total = term if total is None else total + term
        return total

    count = HALF // 2 + 1
    return [one(even_in, j) for j in range(count)], [one(odd_in, j) for j in range(count)]


def half_transform(values, use_cos):
    even = [(i, v) for i, v in values.items() if i % 2 == 0]
    odd = [(i, v) for i, v in values.items() if i % 2 == 1]
    es, os_ = dft_even_odd(even, odd, use_cos)
    zero = jnp.zeros_like(next(iter(values.values())))
    out = {}
    for j in range(HALF // 2 + 1):
        e = zero if es[j] is None else es[j]
        o = zero if os_[j] is None else os_[j]
        out[j] = e + o
        out[HALF - j] = (e - o) if use_cos else (o - e)
    return out


def step_kernel(zn, dp, window, *refs):
    (refs_ref, part_ref, row_ref, focus_ref, cw_ref, prior_ref,
     out_ref, inv_ref, ev_ref,
     part, both, held, cres, energy, sbuf, psum, pp, rows2, table,
     stat, stat_got, mass, mslots,
     xsend, xrecv, zsend, zrecv, xlast, esend, erecv, sib, acc, finx, finz,
     psem, keep, ksend, krecv, wsend, wrecv, rsend, rrecv,
     ax_s, ax_r, az_s, az_r, ae_s, ae_r, ssend, srecv, msend, mrecv,
     rx_s, rx_r, rz_s, rz_r, re_s, re_r, fx_r, fz_r, bsend, brecv) = refs
    me = lax.axis_index("dp")
    z, x, c = me // 4, (me // 2) % 2, me % 2
    o = 1 - c
    y = 1 - x
    n = part.shape[0]
    m_all, q = both.shape[0], both.shape[-1]
    mb, kh = held.shape[2], held.shape[3]
    k = 2 * kh
    n2 = 2 * n
    nall = n * dp
    end = zn - 1

    def at(zz, xx, cc):
        return zz * 4 + xx * 2 + cc

    def chip(zz, xx):
        return zz * 2 + xx

    def remote(src, dst, ss, rs, target):
        return pltpu.make_async_remote_copy(
            src_ref=src, dst_ref=dst, send_sem=ss, recv_sem=rs,
            device_id=dev(target), device_id_type=MESH,
        )

    def is_end(zz):
        return jnp.logical_or(zz == 0, zz == end)

    def inside(zz):
        return jnp.logical_and(zz >= 0, zz < zn)

    def sign_of(s):
        return 1 - 2 * s

    def slot(d, s, e):
        return (d * 2 + s) * 2 + e

    sibling = at(z, x, o)

    barrier = pltpu.get_barrier_semaphore()

    def greet(target):
        pl.semaphore_signal(barrier, inc=1, device_id=dev(target), device_id_type=MESH)

    greet(sibling)
    greet(at(z, y, 0))
    greet(at(z, y, 1))
    for zz in (z - 1, z + 1):
        @pl.when(inside(zz))
        def _():
            greet(at(zz, x, 0))
            greet(at(zz, x, 1))

    load = pltpu.make_async_copy(part_ref, part, psem)
    load.start()
    mine = pltpu.make_async_copy(refs_ref.at[:, c], held.at[chip(z, x), c], keep)
    mine.start()

    lane = lax.broadcasted_iota(jnp.int32, (G, q), 1)
    radius = (jnp.where(lane < R, lane, lane - R).astype(F32) + 1.0) / R
    eye = lax.broadcasted_iota(jnp.int32, (G, G), 0) == lax.broadcasted_iota(jnp.int32, (G, G), 1)
    focus = jnp.sum(jnp.where(eye, jnp.broadcast_to(focus_ref[...], (G, G)), 0.0), axis=1, keepdims=True)
    phase = 20.0 * focus * (radius * radius)
    ctf = -(0.995 * jnp.sin(phase) + 0.1 * jnp.cos(phase))
    cw = jnp.concatenate([cw_ref[...], cw_ref[...]], axis=1)
    gain_table = cw * ctf
    power = gain_table * ctf

    onehot = (row_ref[...] == lax.broadcasted_iota(jnp.int32, (G, n), 0)).astype(F32)
    gain = lax.dot_general(
        onehot, gain_table, (((0,), (0,)), ((), ())),
        preferred_element_type=F32, precision=HIGHEST,
    )
    row = row_ref[...].astype(F32)
    rows2[c] = jnp.broadcast_to(jnp.concatenate([row, row], axis=1), rows2.shape[1:])

    pl.semaphore_wait(
        barrier, 3 + 2 * (z > 0).astype(jnp.int32) + 2 * (z < end).astype(jnp.int32)
    )

    here = chip(z, x)

    def first_z(s, e):
        cc = jnp.bitwise_xor(c, e)
        return remote(refs_ref.at[:, cc], held.at[here, c], az_s.at[slot(0, s, e)],
                      az_r.at[slot(1, s, e)], at(z + sign_of(s), x, cc))

    def first_x(e):
        cc = jnp.bitwise_xor(c, e)
        return remote(refs_ref.at[:, cc], held.at[here, c], ax_s.at[slot(0, 0, e)],
                      ax_r.at[slot(0, 0, e)], at(z, y, cc))

    for e in range(2):
        for s in range(2):
            @pl.when(inside(z + sign_of(s)))
            def _():
                first_z(s, e).start()
        first_x(e).start()
    own_half = remote(refs_ref.at[:, o], held.at[here, c], ksend, krecv, sibling)
    own_half.start()
    rows_copy = remote(rows2.at[c], rows2.at[c], rsend, rrecv, sibling)
    rows_copy.start()

    load.wait()
    turn = jnp.where(lax.broadcasted_iota(jnp.int32, (1, 1, q), 2) < R, F32(1.0), F32(-1.0))
    chunk = 16

    def weighted_copy(i):
        span = pl.ds(pl.multiple_of(i * chunk, chunk), chunk)
        return remote(both.at[span, :, c], both.at[span, :, c], wsend.at[i], wrecv.at[i], sibling)

    @pl.loop(0, m_all // chunk)
    def _(i):
        span = pl.ds(pl.multiple_of(i * chunk, chunk), chunk)
        wide = part[:, span, :].astype(F32) * gain[:, None, :]
        w = jnp.swapaxes(wide, 0, 1).astype(BF16)
        both[span, 0, c] = w
        both[span, 1, c] = (pltpu.roll(w.astype(F32), R, 2) * turn).astype(BF16)
        weighted_copy(i).start()

    cres[...] = jnp.zeros_like(cres)
    energy[...] = jnp.zeros_like(energy)
    below = lax.broadcasted_iota(jnp.int32, (window, G), 0) - lax.broadcasted_iota(jnp.int32, (window, G), 1)
    for p in range(dp // 2):
        pick = (below == -((p * n2 * G) // nall)).astype(F32)
        span = jnp.dot(pick, power, precision=HIGHEST, preferred_element_type=F32)
        table[2 * p * window:(2 * p + 1) * window, :] = span
        table[(2 * p + 1) * window:(2 * p + 2) * window, :] = span

    @pl.loop(0, m_all // chunk)
    def _(i):
        weighted_copy(i).wait_recv()

    def products(block, cc):
        total = None
        for i in range(mb):
            m = (block * 2 + cc) * mb + i
            r = lax.rem(m, ROT)
            images = both[m].reshape(2 * n2, q)
            ref = held[block, cc, i]
            cres[r] += lax.dot_general(
                ref, images, (((1,), (1,)), ((), ())), preferred_element_type=F32
            )
            wide = ref.astype(F32)
            total = wide * wide if total is None else total + wide * wide
        energy[...] += total

    def z_copy(d, s, e):
        piece = held.at[chip(z - sign_of(s) * d, x), jnp.bitwise_xor(c, e)]
        return remote(piece, piece, az_s.at[slot(d, s, e)], az_r.at[slot(d + 1, s, e)],
                      at(z + sign_of(s), x, c))

    def z_wait(d, s, e):
        piece = held.at[chip(z - sign_of(s) * d, x), jnp.bitwise_xor(c, e)]
        return remote(piece, piece, az_s.at[slot(d, s, e)], az_r.at[slot(d, s, e)], sibling)

    def x_copy(d, s, e):
        piece = held.at[chip(z - sign_of(s) * d, x), jnp.bitwise_xor(c, e)]
        return remote(piece, piece, ax_s.at[slot(d, s, e)], ax_r.at[slot(d, s, e)], at(z, y, c))

    def x_wait(d, s, e):
        piece = held.at[chip(z - sign_of(s) * d, y), jnp.bitwise_xor(c, e)]
        return remote(piece, piece, ax_s.at[slot(d, s, e)], ax_r.at[slot(d, s, e)], sibling)

    def e_piece(s):
        return held.at[chip(s * end, y), o]

    def e_copy(s):
        piece = e_piece(s)
        return remote(piece, piece, ae_s.at[s], ae_r.at[s], at(z + sign_of(s), x, c))

    def by_x(zo, e):
        return jnp.logical_not(jnp.logical_and(e == 1, is_end(zo)))

    def z_held(d, s):
        return jnp.logical_and(d < zn, inside(z - sign_of(s) * d))

    def x_held(d, s, e):
        far = jnp.logical_and(inside(z - sign_of(s) * d), by_x(z - sign_of(s) * d, e))
        return jnp.logical_or(jnp.logical_and(d > 0, far), jnp.logical_and(d == 0, s == 0))

    own_done = [False]
    mine.wait()
    products(here, c)
    own_half.wait_recv()
    products(here, o)

    @pl.loop(1, zn + 1)
    def _(d):
        @pl.loop(0, 4)
        def _(j):
            e, s = j // 2, j % 2

            @pl.when(z_held(d, s))
            def _():
                zo = z - sign_of(s) * d
                z_wait(d, s, e).wait_recv()

                @pl.when(inside(z + sign_of(s)))
                def _():
                    z_copy(d, s, e).start()

                @pl.when(by_x(zo, e))
                def _():
                    x_copy(d, s, e).start()

                products(chip(zo, x), jnp.bitwise_xor(c, e))

        @pl.loop(0, 4)
        def _(j):
            e, s = j // 2, j % 2

            @pl.when(x_held(d - 1, s, e))
            def _():
                x_wait(d - 1, s, e).wait_recv()
                for t in range(2):
                    @pl.when(jnp.logical_and(jnp.logical_and(d == 1, e == 1), z == t * end))
                    def _():
                        e_copy(t).start()

                products(chip(z - sign_of(s) * (d - 1), y), jnp.bitwise_xor(c, e))

        @pl.loop(0, 2)
        def _(s):
            gone = jnp.where(s == 0, z, end - z)

            @pl.when(jnp.logical_and(gone == d - 1, gone > 0))
            def _():
                e_copy(s).wait_recv()

                @pl.when(gone < end)
                def _():
                    e_copy(s).start()

                products(chip(s * end, y), o)

    rows_copy.wait_recv()
    group = jnp.concatenate([rows2[0, 0:1, :n], rows2[1, 0:1, :n]], axis=1)
    hot_g = (group == lax.broadcasted_iota(jnp.int32, (G, n2), 0).astype(F32)).astype(F32)
    quad = lax.dot_general(
        energy[...], power, (((1,), (1,)), ((), ())), preferred_element_type=F32, precision=HIGHEST,
    )
    norm = jnp.dot(quad, hot_g, precision=HIGHEST, preferred_element_type=F32)
    diag = lax.broadcasted_iota(jnp.int32, (kh, k), 0) + c * kh == lax.broadcasted_iota(jnp.int32, (kh, k), 1)
    prior = jnp.sum(jnp.where(diag, jnp.broadcast_to(prior_ref[...], (kh, k)), 0.0), axis=1, keepdims=True)
    psum[...] = jnp.log(prior) - 0.5 * norm

    rows = 16

    def score_rows(i, top):
        span = pl.ds(pl.multiple_of(i * rows, rows), rows)
        re, im = pl.ds(0, n2), pl.ds(n2, n2)
        a = {0: cres[0, span, re], HALF: cres[HALF, span, re]}
        b = {}
        for r in range(1, HALF):
            a[r] = cres[r, span, re] + cres[ROT - r, span, re]
            b[r] = cres[r, span, im] - cres[ROT - r, span, im]
        cosine = half_transform(a, True)
        sine = half_transform(b, False)
        add = psum[span, :]
        for j in range(NC):
            base = cosine[j] + add
            if j in (0, HALF):
                sbuf[j, span, :] = base
                top = jnp.maximum(top, base)
            else:
                low, high = base - sine[j], base + sine[j]
                sbuf[j, span, :] = low
                sbuf[ROT - j, span, :] = high
                top = jnp.maximum(top, jnp.maximum(low, high))
        return top

    top = lax.fori_loop(0, kh // rows, score_rows, jnp.full((rows, n2), -jnp.inf, F32))
    top = jnp.max(top, axis=0, keepdims=True)

    def exp_rows(i, total):
        span = pl.ds(pl.multiple_of(i * rows, rows), rows)
        part_sum = None
        for j in range(ROT):
            value = jnp.exp(sbuf[j, span, :] - top)
            sbuf[j, span, :] = value
            part_sum = value if part_sum is None else part_sum + value
        psum[span, :] = part_sum
        return total + part_sum

    total = lax.fori_loop(0, kh // rows, exp_rows, jnp.zeros((rows, n2), F32))
    total = jnp.sum(total, axis=0, keepdims=True)
    which = lax.broadcasted_iota(jnp.int32, stat.shape, 0)
    stat[...] = jnp.where(which == 0, top, total)
    stat_copy = remote(stat, stat_got, ssend, srecv, sibling)
    stat_copy.start()
    stat_copy.wait_recv()
    other_top, other_total = stat_got[0:1, :], stat_got[1:2, :]
    most = jnp.maximum(top, other_top)
    shrink = jnp.exp(top - most)
    whole = total * shrink + other_total * jnp.exp(other_top - most)
    evidence = most + jnp.log(whole)
    ev_ref[...] = jnp.where(c == 0, evidence[:, :n], evidence[:, n:])
    scale = shrink / whole

    @pl.loop(0, kh // rows)
    def _(i):
        span = pl.ds(pl.multiple_of(i * rows, rows), rows)
        u = {0: sbuf[0, span, :] * scale, HALF: sbuf[HALF, span, :] * scale}
        v = {}
        for j in range(1, HALF):
            low, high = sbuf[j, span, :], sbuf[ROT - j, span, :]
            u[j] = (low + high) * scale
            v[j] = (low - high) * scale
        real = half_transform(u, True)
        imag = half_transform(v, False)
        for r in range(NC):
            re = real[r].astype(BF16)
            im = imag[r].astype(BF16)
            pp[r, span, 0:n2] = re
            pp[r, span, n2:] = -im
            if 0 < r < HALF:
                pp[ROT - r, span, 0:n2] = re
                pp[ROT - r, span, n2:] = im

    def numer(block, cc, i):
        m = (block * 2 + cc) * mb + i
        r = lax.rem(m, ROT)
        return jnp.dot(pp[r], both[m].reshape(2 * n2, q), preferred_element_type=F32)

    def e_sum(s):
        return remote(esend.at[s], erecv.at[s], re_s.at[s], re_r.at[s], at(z + sign_of(s), x, c))

    for s in range(2):
        @pl.when(z == s * end)
        def _():
            for i in range(mb):
                esend[s, i] = numer(chip(end - s * end, y), o, i).astype(BF16)
            e_sum(s).start()

    def x_sum(d, s, e):
        return remote(xsend.at[slot(d, s, e)], xrecv.at[slot(d, s, e)],
                      rx_s.at[slot(d, s, e)], rx_r.at[slot(d, s, e)], at(z, y, c))

    def x_last(e):
        return remote(xlast.at[e], finx.at[c], rx_s.at[slot(0, 0, e)], fx_r.at[c],
                      at(z, y, jnp.bitwise_xor(c, e)))

    def x_goes(d, s, e):
        zo = z + sign_of(s) * d
        return jnp.logical_and(inside(zo), by_x(zo, e))

    @pl.loop(0, zn - 1)
    def _(t):
        d = end - t

        @pl.loop(0, 4)
        def _(j):
            e, s = j // 2, j % 2

            @pl.when(x_goes(d, s, e))
            def _():
                for i in range(mb):
                    xsend[slot(d, s, e), i] = numer(
                        chip(z + sign_of(s) * d, y), jnp.bitwise_xor(c, e), i
                    ).astype(BF16)
                x_sum(d, s, e).start()

    def send_last(e, extra):
        for i in range(mb):
            value = numer(chip(z, y), jnp.bitwise_xor(c, e), i)
            if extra is not None:
                value = value + erecv[extra, i].astype(F32)
            xlast[e, i] = value.astype(BF16)
        x_last(e).start()

    @pl.loop(0, 2)
    def _(e):
        @pl.when(by_x(z, e))
        def _():
            send_last(e, None)

    start = (here * n2 * G) // nall
    hot = (
        group == (lax.broadcasted_iota(jnp.int32, (window, n2), 0) + start).astype(F32)
    ).astype(F32)
    part_mass = lax.dot_general(
        hot, psum[...] * scale, (((1,), (1,)), ((), ())), preferred_element_type=F32, precision=HIGHEST,
    )
    nothing = jnp.zeros_like(part_mass)
    mass[...] = jnp.where(
        c == 0, jnp.concatenate([part_mass, nothing], axis=1), jnp.concatenate([nothing, part_mass], axis=1)
    )
    mslots[me] = mass[...]

    def mass_copy(g):
        return remote(mass, mslots.at[me], msend.at[g], mrecv.at[g], lax.rem(me + g, dp))

    def mass_wait(g):
        return remote(mass, mslots.at[lax.rem(me + dp - g, dp)], msend.at[g], mrecv.at[g], sibling)

    @pl.loop(1, dp)
    def _(g):
        mass_copy(g).start()

    for i in range(mb):
        sib[i] = numer(here, o, i)
    sib_copy = remote(sib, acc.at[c], bsend, brecv, sibling)
    sib_copy.start()

    def z_sum(d, s, e):
        return remote(zsend.at[slot(d, s, e)], zrecv.at[slot(d - 1, s, e)],
                      rz_s.at[slot(d, s, e)], rz_r.at[slot(d - 1, s, e)], at(z + sign_of(s), x, c))

    def z_got(d, s, e):
        return remote(zsend.at[slot(d, s, e)], zrecv.at[slot(d, s, e)],
                      rz_s.at[slot(d, s, e)], rz_r.at[slot(d, s, e)], sibling)

    def z_last(s, e):
        return remote(zsend.at[slot(1, s, e)], finz.at[s, c], rz_s.at[slot(1, s, e)], fz_r.at[s, c],
                      at(z + sign_of(s), x, jnp.bitwise_xor(c, e)))

    near = (2 * z < zn).astype(jnp.int32)

    @pl.loop(0, zn - 1)
    def _(t):
        d = end - t

        for s in range(2):
            left = (end - z) if s == 0 else z

            @pl.when(jnp.logical_and(left == d, left < end))
            def _():
                e_sum(s).wait_recv()
                for i in range(mb):
                    esend[s, i] = (numer(chip(end - s * end, y), o, i) + erecv[s, i].astype(F32)).astype(BF16)
                e_sum(s).start()

        for s in range(2):
            @pl.when(jnp.logical_and(d == 1, z == (1 - s) * end))
            def _():
                e_sum(s).wait_recv()
                send_last(1, s)

        @pl.loop(0, 4)
        def _(j):
            e = 1 - j // 2
            s = jnp.bitwise_xor(j % 2, near)
            zo = z + sign_of(s) * d

            @pl.when(inside(zo))
            def _():
                here_slot = slot(d, s, e)
                crossed = by_x(zo, e)
                line = inside(z - sign_of(s))
                for i in range(mb):
                    acc[c, i] = numer(chip(zo, x), jnp.bitwise_xor(c, e), i)

                @pl.when(crossed)
                def _():
                    x_sum(d, s, e).wait_recv()
                    for i in range(mb):
                        acc[c, i] += xrecv[here_slot, i].astype(F32)

                @pl.when(line)
                def _():
                    z_got(d, s, e).wait_recv()
                    for i in range(mb):
                        acc[c, i] += zrecv[here_slot, i].astype(F32)

                for i in range(mb):
                    zsend[here_slot, i] = acc[c, i].astype(BF16)

                @pl.when(d > 1)
                def _():
                    z_sum(d, s, e).start()

                @pl.when(d == 1)
                def _():
                    z_last(s, e).start()

    for i in range(mb):
        acc[c, i] = numer(here, c, i)

    @pl.loop(1, dp)
    def _(g):
        mass_wait(g).wait_recv()

    denom = 1.0 + lax.dot_general(
        mslots[...].reshape(dp * window, k), table[...], (((0,), (0,)), ((), ())),
        preferred_element_type=F32, precision=HIGHEST,
    )
    inv_ref[...] = (1.0 / denom).reshape(inv_ref.shape)
    sib_copy.wait_recv()

    for h in range(2):
        remote(xlast.at[0], finx.at[h], rx_s.at[slot(0, 0, 0)], fx_r.at[h], sibling).wait_recv()
        acc[h] += finx[h].astype(F32)
    for s in range(2):
        @pl.when(inside(z - sign_of(s)))
        def _():
            for h in range(2):
                remote(xlast.at[0], finz.at[s, h], rx_s.at[slot(0, 0, 0)], fz_r.at[s, h], sibling).wait_recv()
                acc[h] += finz[s, h].astype(F32)
    for h in range(2):
        out_ref[:, h] = acc[h]

    for e in range(2):
        for s in range(2):
            @pl.when(inside(z + sign_of(s)))
            def _():
                first_z(s, e).wait_send()
        first_x(e).wait_send()
    own_half.wait_send()
    rows_copy.wait_send()
    stat_copy.wait_send()
    sib_copy.wait_send()

    @pl.loop(0, m_all // chunk)
    def _(i):
        weighted_copy(i).wait_send()

    @pl.loop(1, zn)
    def _(d):
        @pl.loop(0, 4)
        def _(j):
            e, s = j // 2, j % 2
            zo = z - sign_of(s) * d

            @pl.when(z_held(d, s))
            def _():
                @pl.when(inside(z + sign_of(s)))
                def _():
                    z_copy(d, s, e).wait_send()

                @pl.when(by_x(zo, e))
                def _():
                    x_copy(d, s, e).wait_send()

            @pl.when(x_goes(d, s, e))
            def _():
                x_sum(d, s, e).wait_send()

            @pl.when(inside(z + sign_of(s) * d))
            def _():
                z_got(d, s, e).wait_send()

    for s in range(2):
        @pl.when(inside(z + sign_of(s)))
        def _():
            e_copy(s).wait_send()
            e_sum(s).wait_send()
    for e in range(2):
        x_last(e).wait_send()

    @pl.loop(1, dp)
    def _(g):
        mass_copy(g).wait_send()


def finish_kernel(total_ref, inv_ref, ev_ref, out_ref, evidence_ref):
    for i in range(total_ref.shape[0]):
        out_ref[i] = total_ref[i] * inv_ref[...]
    evidence_ref[...] = ev_ref[...]


def shards(dp, particles, refs, ctf_group, defocus, class_prior, cycle_weight):
    n, m_all, q = particles.shape
    mb, k, _ = refs.shape
    zn = dp // 4
    nall = n * dp
    kh = k // 2
    n2 = 2 * n
    window = -(-((n2 * G) // nall + 3) // 8) * 8
    slots = 4 * zn
    weighted_chunks = m_all // 16

    vmem = pl.BlockSpec(memory_space=pltpu.VMEM)
    hbm = pl.BlockSpec(memory_space=pl.ANY)
    sem = pltpu.SemaphoreType.DMA
    total, inv, ev = pl.pallas_call(
        functools.partial(step_kernel, zn, dp, window),
        out_shape=(
            jax.ShapeDtypeStruct((mb, 2, kh, q), F32),
            jax.ShapeDtypeStruct((2, kh, q), F32),
            jax.ShapeDtypeStruct((1, n), F32),
        ),
        in_specs=[hbm, hbm] + [vmem] * 4,
        out_specs=(vmem, vmem, vmem),
        scratch_shapes=[
            pltpu.VMEM((n, m_all, q), BF16),
            pltpu.VMEM((m_all, 2, 2, n, q), BF16),
            pltpu.VMEM((dp // 2, 2, mb, kh, q), BF16),
            pltpu.VMEM((ROT, kh, 2 * n2), F32),
            pltpu.VMEM((kh, q), F32),
            pltpu.VMEM((ROT, kh, n2), F32),
            pltpu.VMEM((kh, n2), F32),
            pltpu.VMEM((ROT, kh, 2 * n2), BF16),
            pltpu.VMEM((2, 8, n2), F32),
            pltpu.VMEM((dp * window, q), F32),
            pltpu.VMEM((8, n2), F32),
            pltpu.VMEM((8, n2), F32),
            pltpu.VMEM((window, k), F32),
            pltpu.VMEM((dp, window, k), F32),
            pltpu.VMEM((slots, mb, kh, q), BF16),
            pltpu.VMEM((slots, mb, kh, q), BF16),
            pltpu.VMEM((slots, mb, kh, q), BF16),
            pltpu.VMEM((slots, mb, kh, q), BF16),
            pltpu.VMEM((2, mb, kh, q), BF16),
            pltpu.VMEM((2, mb, kh, q), BF16),
            pltpu.VMEM((2, mb, kh, q), BF16),
            pltpu.VMEM((mb, kh, q), F32),
            pltpu.VMEM((2, mb, kh, q), F32),
            pltpu.VMEM((2, mb, kh, q), BF16),
            pltpu.VMEM((2, 2, mb, kh, q), BF16),
            sem, sem, sem, sem, sem((weighted_chunks,)), sem((weighted_chunks,)), sem, sem,
            sem((slots,)), sem((slots,)), sem((slots,)), sem((slots + 4,)), sem((2,)), sem((2,)),
            sem, sem, sem((dp,)), sem((dp,)),
            sem((slots,)), sem((slots,)), sem((slots,)), sem((slots,)), sem((2,)), sem((2,)),
            sem((2,)), sem((2, 2)), sem, sem,
        ],
        compiler_params=pltpu.CompilerParams(collective_id=0, has_side_effects=True),
        name="step",
    )(
        refs.reshape(mb, 2, kh, q), particles, ctf_group[None, :], defocus[None, :],
        cycle_weight[None, :], class_prior[None, :],
    )

    new_refs, evidence = pl.pallas_call(
        finish_kernel,
        out_shape=(
            jax.ShapeDtypeStruct((mb, 2, kh, q), F32),
            jax.ShapeDtypeStruct((1, n), F32),
        ),
        in_specs=[vmem] * 3,
        out_specs=(vmem, vmem),
        name="finish",
    )(total, inv, ev)
    return (new_refs.reshape(mb, k, q), evidence[0])


def solution(mesh):
    in_specs = (
        P(("groups", "dp"), None, None),
        P("dp", "groups", None),
        P(("groups", "dp")),
        P("groups"),
        P("groups"),
        P(),
    )
    out_specs = (P("dp", "groups", None), P(("groups", "dp")))
    return jax.shard_map(
        functools.partial(shards, mesh.shape["dp"]),
        mesh=mesh, in_specs=in_specs, out_specs=out_specs, check_vma=False,
    )
```

time: 80.7 us -> 64.9 us (0.80)
  Pallas kernels: 77.5 us -> 64 us
  local copies, waits for them, and re-layouts: 2.39 us -> 0 us
    pallas_call x2, Pallas kernels: 77.5 us -> 64 us  [the longest x1 62.1 us: shards(): pl.pallas_call(functools.partial(step_kernel, zn, dp, window), out_shape=...]
    unnamed x4 -> x0, local copies, waits for them, and re-layouts: 2.39 us -> none
where the time goes in v2:
time: 64.9 us; the launch traced here: 64.7 us
  Pallas kernels  64 us (99%)
    pallas_call x1, Pallas kernels, shards(): pl.pallas_call(functools.partial(step_kernel, zn, dp, window), out_shape=...  62.1 us
    pallas_call x1, Pallas kernels, shards(): pl.pallas_call(finish_kernel, out_shape=(jax.ShapeDtypeStruct((mb, 2, kh,...  1.92 us

profile of v2, /device:TPU:0, one launch (start us, length us, event | category | flops | bytes accessed | tf_op | source)
XLA Modules:
  0.0 64.7 jit_solution(476600295520179080)
XLA Ops:
  0.6 62.1 %step.1 = (f32[8,2,64,128]{3,2,1,0:T(8,128)}, f32[2,64,128]{2,1,0:T(8,128)}, f32[1,64]{1,0:T(1,128)}) custom-call(bf16[8,2,64,128]{3,2,1,0:T(8,128)(2,1)} %bitcast.7, bf16[64,128,128]{2,1,0:T(8,128)(2,1)} %refs_1_.1, s32[1,64]{1,0:T(1,128)} %bitcast.8, f32[1,32]{1,0:T(1,128)} %bitcast.9, f32[1,64]{1,0:T(1,128)} %bitcast.10, f32[1,128]{1,0:T(1,128)} %bitcast.11), custom_call_target="tpu_custom_call" | custom-call | tf_op jit(solution)/shard_map/step/pallas_call | solution.py:645
  62.8 1.9 %finish.1 = (f32[8,2,64,128]{3,2,1,0:T(8,128)}, f32[1,64]{1,0:T(1,128)}) custom-call(f32[8,2,64,128]{3,2,1,0:T(8,128)} %get-tuple-element.7.total_ref, f32[2,64,128]{2,1,0:T(8,128)} %get-tuple-element.8.inv_ref, f32[1,64]{1,0:T(1,128)} %get-tuple-element.9.ev_ref), custom_call_target="tpu_custom_call" | custom-call | tf_op jit(solution)/shard_map/finish/pallas_call | solution.py:693

commit v3 on v2

--- a/solution.py
+++ b/solution.py
@@ -60,9 +60,9 @@
 
 
 def step_kernel(zn, dp, window, *refs):
-    (refs_ref, part_ref, row_ref, focus_ref, cw_ref, prior_ref,
+    (refs_ref, part_ref, row_hbm, focus_hbm, cw_hbm, prior_hbm,
      out_ref, inv_ref, ev_ref,
-     part, both, held, cres, energy, sbuf, psum, pp, rows2, table,
+     row_ref, focus_ref, cw_ref, prior_ref, small, part, both, held, cres, energy, sbuf, psum, pp, rows2, table,
      stat, stat_got, mass, mslots,
      xsend, xrecv, zsend, zrecv, xlast, esend, erecv, sib, acc, finx, finz,
      psem, keep, ksend, krecv, wsend, wrecv, rsend, rrecv,
@@ -120,11 +120,21 @@
             greet(at(zz, x, 0))
             greet(at(zz, x, 1))
 
+    smalls = [
+        pltpu.make_async_copy(a, b, small.at[i])
+        for i, (a, b) in enumerate((
+            (row_hbm, row_ref), (focus_hbm, focus_ref), (cw_hbm, cw_ref), (prior_hbm, prior_ref)
+        ))
+    ]
+    for copy in smalls:
+        copy.start()
     load = pltpu.make_async_copy(part_ref, part, psem)
     load.start()
     mine = pltpu.make_async_copy(refs_ref.at[:, c], held.at[chip(z, x), c], keep)
     mine.start()
 
+    for copy in smalls:
+        copy.wait()
     lane = lax.broadcasted_iota(jnp.int32, (G, q), 1)
     radius = (jnp.where(lane < R, lane, lane - R).astype(F32) + 1.0) / R
     eye = lax.broadcasted_iota(jnp.int32, (G, G), 0) == lax.broadcasted_iota(jnp.int32, (G, G), 1)
@@ -195,10 +205,6 @@
         span = jnp.dot(pick, power, precision=HIGHEST, preferred_element_type=F32)
         table[2 * p * window:(2 * p + 1) * window, :] = span
         table[(2 * p + 1) * window:(2 * p + 2) * window, :] = span
-
-    @pl.loop(0, m_all // chunk)
-    def _(i):
-        weighted_copy(i).wait_recv()
 
     def products(block, cc):
         total = None
@@ -248,37 +254,28 @@
         far = jnp.logical_and(inside(z - sign_of(s) * d), by_x(z - sign_of(s) * d, e))
         return jnp.logical_or(jnp.logical_and(d > 0, far), jnp.logical_and(d == 0, s == 0))
 
-    own_done = [False]
-    mine.wait()
-    products(here, c)
-    own_half.wait_recv()
-    products(here, o)
-
-    @pl.loop(1, zn + 1)
-    def _(d):
-        @pl.loop(0, 4)
-        def _(j):
-            e, s = j // 2, j % 2
-
+    def z_forward(d, s, e):
+        @pl.when(z_held(d, s))
+        def _():
+            z_wait(d, s, e).wait_recv()
+
+            @pl.when(inside(z + sign_of(s)))
+            def _():
+                z_copy(d, s, e).start()
+
+            @pl.when(by_x(z - sign_of(s) * d, e))
+            def _():
+                x_copy(d, s, e).start()
+
+    def half_step(d, e):
+        @pl.loop(0, 2)
+        def _(s):
             @pl.when(z_held(d, s))
             def _():
-                zo = z - sign_of(s) * d
-                z_wait(d, s, e).wait_recv()
-
-                @pl.when(inside(z + sign_of(s)))
-                def _():
-                    z_copy(d, s, e).start()
-
-                @pl.when(by_x(zo, e))
-                def _():
-                    x_copy(d, s, e).start()
-
-                products(chip(zo, x), jnp.bitwise_xor(c, e))
-
-        @pl.loop(0, 4)
-        def _(j):
-            e, s = j // 2, j % 2
-
+                products(chip(z - sign_of(s) * d, x), jnp.bitwise_xor(c, e))
+
+        @pl.loop(0, 2)
+        def _(s):
             @pl.when(x_held(d - 1, s, e))
             def _():
                 x_wait(d - 1, s, e).wait_recv()
@@ -289,19 +286,44 @@
 
                 products(chip(z - sign_of(s) * (d - 1), y), jnp.bitwise_xor(c, e))
 
+    mine.wait()
+
+    @pl.loop(1, zn + 1)
+    def _(d):
         @pl.loop(0, 2)
-        def _(s):
-            gone = jnp.where(s == 0, z, end - z)
-
-            @pl.when(jnp.logical_and(gone == d - 1, gone > 0))
-            def _():
-                e_copy(s).wait_recv()
-
-                @pl.when(gone < end)
-                def _():
-                    e_copy(s).start()
-
-                products(chip(s * end, y), o)
+        def _(e):
+            for s in range(2):
+                z_forward(d, s, e)
+
+            @pl.when(jnp.logical_and(d == 1, e == 0))
+            def _():
+                @pl.loop(0, m_all // chunk)
+                def _(i):
+                    weighted_copy(i).wait_recv()
+
+                own_half.wait_recv()
+
+                @pl.loop(0, 2)
+                def _(cc):
+                    products(here, cc)
+
+            half_step(d, e)
+
+            @pl.when(e == 0)
+            def _():
+                @pl.loop(0, 2)
+                def _(s):
+                    gone = jnp.where(s == 0, z, end - z)
+
+                    @pl.when(jnp.logical_and(gone == d - 1, gone > 0))
+                    def _():
+                        e_copy(s).wait_recv()
+
+                        @pl.when(gone < end)
+                        def _():
+                            e_copy(s).start()
+
+                        products(chip(s * end, y), o)
 
     rows_copy.wait_recv()
     group = jnp.concatenate([rows2[0, 0:1, :n], rows2[1, 0:1, :n]], axis=1)
@@ -622,10 +644,16 @@
         mass_copy(g).wait_send()
 
 
-def finish_kernel(total_ref, inv_ref, ev_ref, out_ref, evidence_ref):
+def finish_kernel(total_ref, inv_ref, ev_ref, out_ref, evidence_ref, buf, sems):
+    copies = []
     for i in range(total_ref.shape[0]):
-        out_ref[i] = total_ref[i] * inv_ref[...]
+        buf[i] = total_ref[i] * inv_ref[...]
+        copy = pltpu.make_async_copy(buf.at[i], out_ref.at[i], sems.at[i])
+        copy.start()
+        copies.append(copy)
     evidence_ref[...] = ev_ref[...]
+    for copy in copies:
+        copy.wait()
 
 
 def shards(dp, particles, refs, ctf_group, defocus, class_prior, cycle_weight):
@@ -649,9 +677,11 @@
             jax.ShapeDtypeStruct((2, kh, q), F32),
             jax.ShapeDtypeStruct((1, n), F32),
         ),
-        in_specs=[hbm, hbm] + [vmem] * 4,
+        in_specs=[pl.BlockSpec(memory_space=pltpu.MemorySpace.HBM)] * 6,
         out_specs=(vmem, vmem, vmem),
         scratch_shapes=[
+            pltpu.VMEM((1, n), jnp.int32), pltpu.VMEM((1, G), F32),
+            pltpu.VMEM((1, R), F32), pltpu.VMEM((1, k), F32), sem((4,)),
             pltpu.VMEM((n, m_all, q), BF16),
             pltpu.VMEM((m_all, 2, 2, n, q), BF16),
             pltpu.VMEM((dp // 2, 2, mb, kh, q), BF16),
@@ -683,12 +713,16 @@
             sem((slots,)), sem((slots,)), sem((slots,)), sem((slots,)), sem((2,)), sem((2,)),
             sem((2,)), sem((2, 2)), sem, sem,
         ],
-        compiler_params=pltpu.CompilerParams(collective_id=0, has_side_effects=True),
+        compiler_params=pltpu.CompilerParams(
+            collective_id=0, has_side_effects=True, vmem_limit_bytes=40 << 20
+        ),
         name="step",
-    )(
-        refs.reshape(mb, 2, kh, q), particles, ctf_group[None, :], defocus[None, :],
-        cycle_weight[None, :], class_prior[None, :],
-    )
+    )(*(
+        pltpu.with_memory_space_constraint(a, pltpu.MemorySpace.HBM) for a in (
+            refs.reshape(mb, 2, kh, q), particles, ctf_group[None, :], defocus[None, :],
+            cycle_weight[None, :], class_prior[None, :],
+        )
+    ))
 
     new_refs, evidence = pl.pallas_call(
         finish_kernel,
@@ -697,7 +731,9 @@
             jax.ShapeDtypeStruct((1, n), F32),
         ),
         in_specs=[vmem] * 3,
-        out_specs=(vmem, vmem),
+        out_specs=(hbm, vmem),
+        scratch_shapes=[pltpu.VMEM((mb, 2, kh, q), F32), sem((mb,))],
+        compiler_params=pltpu.CompilerParams(vmem_limit_bytes=8 << 20),
         name="finish",
     )(total, inv, ev)
     return (new_refs.reshape(mb, k, q), evidence[0])

time: 64.9 us -> 59.1 us (0.911)
  Pallas kernels: 64 us -> 58.3 us
    pallas_call x1, Pallas kernels: 62.1 us -> 57 us  [shards(): pl.pallas_call(functools.partial(step_kernel, zn, dp, window), out_shape=...]
where the time goes in v3:
time: 59.1 us; the launch traced here: 59 us
  Pallas kernels  58.3 us (99%)
  between operations  0.64 us (1%)
    pallas_call x1, Pallas kernels, shards(): pl.pallas_call(functools.partial(step_kernel, zn, dp, window), out_shape=...  57 us
    pallas_call x1, Pallas kernels, shards(): pl.pallas_call(finish_kernel, out_shape=(jax.ShapeDtypeStruct((mb, 2, kh,...  1.37 us

profile of v3, /device:TPU:0, one launch (start us, length us, event | category | flops | bytes accessed | tf_op | source)
XLA Modules:
  0.0 59.0 jit_solution(1305971221702681481)
XLA Ops:
  0.6 57.0 %step.1 = (f32[8,2,64,128]{3,2,1,0:T(8,128)S(1)}, f32[2,64,128]{2,1,0:T(8,128)S(1)}, f32[1,64]{1,0:T(1,128)S(1)}) custom-call(bf16[8,2,64,128]{3,2,1,0:T(8,128)(2,1)} %bitcast.7, bf16[64,128,128]{2,1,0:T(8,128)(2,1)} %refs_1_.1, s32[1,64]{1,0:T(1,128)} %bitcast.8, f32[1,32]{1,0:T(1,128)} %bitcast.9, f32[1,64]{1,0:T(1,128)} %bitcast.10, f32[1,128]{1,0:T(1,128)} %bitcast.11), custom_call_target="tpu_custom_call" | custom-call | tf_op jit(solution)/shard_map/step/pallas_call | solution.py:673
  57.6 1.4 %finish.1 = (f32[8,2,64,128]{3,2,1,0:T(8,128)}, f32[1,64]{1,0:T(1,128)}) custom-call(f32[8,2,64,128]{3,2,1,0:T(8,128)S(1)} %get-tuple-element.7.total_ref, f32[2,64,128]{2,1,0:T(8,128)S(1)} %get-tuple-element.8.inv_ref, f32[1,64]{1,0:T(1,128)S(1)} %get-tuple-element.9.ev_ref), custom_call_target="tpu_custom_call" | custom-call | tf_op jit(solution)/shard_map/finish/pallas_call | solution.py:727

commit v4 on v3

--- a/solution.py
+++ b/solution.py
@@ -23,46 +23,95 @@
     return {"dp": index}
 
 
-def dft_even_odd(even_in, odd_in, use_cos):
-    f = math.cos if use_cos else math.sin
-
-    def one(items, j):
-        total = None
-        for i, v in items:
-            w = f(2.0 * math.pi * ((i * j) % ROT) / ROT)
-            if abs(w) < 1e-12:
-                continue
-            if abs(w - 1.0) < 1e-12:
-                term = v
-            elif abs(w + 1.0) < 1e-12:
-                term = -v
-            else:
-                term = v * jnp.float32(w)
-            total = term if total is None else total + term
-        return total
-
-    count = HALF // 2 + 1
-    return [one(even_in, j) for j in range(count)], [one(odd_in, j) for j in range(count)]
-
-
-def half_transform(values, use_cos):
-    even = [(i, v) for i, v in values.items() if i % 2 == 0]
-    odd = [(i, v) for i, v in values.items() if i % 2 == 1]
-    es, os_ = dft_even_odd(even, odd, use_cos)
-    zero = jnp.zeros_like(next(iter(values.values())))
+def cosine9(x, a):
+    c1, c2, c4 = (jnp.float32(math.cos(2.0 * math.pi * p / 9)) for p in (1, 2, 4))
+    a1, a2, a3, a4 = a
+    both = a1 + a2 + a4
+    near = x + a3
+    base = x - a3 * jnp.float32(0.5)
+    d1, d2 = a1 - a4, a2 - a4
+    y1 = c1 * d1 + c2 * d2
+    y2 = c2 * d1 + c4 * d2
+    return [near + both, base + y1, base + y2, near - both * jnp.float32(0.5), base - (y1 + y2)]
+
+
+def sine9(b):
+    s1, s4 = (jnp.float32(math.sin(2.0 * math.pi * p / 9)) for p in (1, 4))
+    half = jnp.float32(math.sqrt(3.0) / 2.0)
+    b1, b2, b3, b4 = b
+    e1, e2 = b1 + b2, b2 + b4
+    e3 = b1 - b4
+    t = half * b3
+    z1 = s1 * e1 + s4 * e2
+    z2 = s1 * e3 + s4 * e1
+    return [z1 + t, z2 - t, half * (b1 - b2 + b4), (z2 - z1) + t]
+
+
+def turns(real, imag):
+    a = {r: real(r) + real(ROT - r) for r in range(1, ROT) if r % 9 in (1, 2, 3, 4)}
+    b = {r: imag(r) - imag(ROT - r) for r in a}
+    a9, b9 = real(9) + real(27), imag(9) - imag(27)
+    first, last = real(0), real(18)
+    up, down = first + last, first - last
+    flat = [up + a9, down - b9, up - a9, down + b9]
+    cos_in, sin_in = [[], [], [], []], [[], [], [], []]
+    for p in range(1, 5):
+        r = [(9 * i + 28 * p) % ROT for i in range(4)]
+        re, im = [a[v] for v in r], [b[v] for v in r]
+        re02, re13, im02, im13 = re[0] + re[2], re[1] + re[3], im[0] + im[2], im[1] + im[3]
+        dr02, dr13, di02, di13 = re[0] - re[2], re[1] - re[3], im[0] - im[2], im[1] - im[3]
+        for t, v in enumerate((re02 + re13, dr02 - di13, re02 - re13, dr02 + di13)):
+            cos_in[t].append(v)
+        for t, v in enumerate((im02 + im13, di02 + dr13, im02 - im13, di02 - dr13)):
+            sin_in[t].append(v)
     out = {}
-    for j in range(HALF // 2 + 1):
-        e = zero if es[j] is None else es[j]
-        o = zero if os_[j] is None else os_[j]
-        out[j] = e + o
-        out[HALF - j] = (e - o) if use_cos else (o - e)
+    for t in range(4):
+        cosine, sine = cosine9(flat[t], cos_in[t]), sine9(sin_in[t])
+        out[(9 * t) % ROT] = cosine[0]
+        for g in range(1, 5):
+            out[(9 * t + 4 * g) % ROT] = cosine[g] - sine[g - 1]
+            out[(9 * t + 4 * (9 - g)) % ROT] = cosine[g] + sine[g - 1]
     return out
+
+
+def harmonics(value):
+    real, imag = [], []
+    for t in range(4):
+        v = [value((9 * t + 4 * g) % ROT) for g in range(9)]
+        real.append(cosine9(v[0], [v[g] + v[9 - g] for g in range(1, 5)]))
+        imag.append(sine9([v[g] - v[9 - g] for g in range(1, 5)]))
+    re, im = {}, {}
+
+    def put(r, x, y):
+        if r <= HALF:
+            re[r] = x
+            if y is not None:
+                im[r] = y
+        else:
+            re[ROT - r] = x
+            if y is not None:
+                im[ROT - r] = -y
+
+    x = [real[t][0] for t in range(4)]
+    put(0, (x[0] + x[2]) + (x[1] + x[3]), None)
+    put(18, (x[0] + x[2]) - (x[1] + x[3]), None)
+    put(9, x[0] - x[2], x[1] - x[3])
+    for p in range(1, 5):
+        x = [real[t][p] for t in range(4)]
+        y = [imag[t][p - 1] for t in range(4)]
+        sx, tx, sy, ty = x[0] + x[2], x[1] + x[3], y[0] + y[2], y[1] + y[3]
+        dx, ex, dy, ey = x[0] - x[2], x[1] - x[3], y[0] - y[2], y[1] - y[3]
+        put((28 * p) % ROT, sx + tx, sy + ty)
+        put((9 + 28 * p) % ROT, dx - ey, dy + ex)
+        put((18 + 28 * p) % ROT, sx - tx, sy - ty)
+        put((27 + 28 * p) % ROT, dx + ey, dy - ex)
+    return re, im
 
 
 def step_kernel(zn, dp, window, *refs):
     (refs_ref, part_ref, row_hbm, focus_hbm, cw_hbm, prior_hbm,
-     out_ref, inv_ref, ev_ref,
-     row_ref, focus_ref, cw_ref, prior_ref, small, part, both, held, cres, energy, sbuf, psum, pp, rows2, table,
+     out_ref, ev_ref,
+     inv, row_ref, focus_ref, cw_ref, prior_ref, small, part, both, held, cres, energy, sbuf, psum, pp, rows2, table,
      stat, stat_got, mass, mslots,
      xsend, xrecv, zsend, zrecv, xlast, esend, erecv, sib, acc, finx, finz,
      psem, keep, ksend, krecv, wsend, wrecv, rsend, rrecv,
@@ -267,13 +316,14 @@
             def _():
                 x_copy(d, s, e).start()
 
-    def half_step(d, e):
+    def half_step_z(d, e):
         @pl.loop(0, 2)
         def _(s):
             @pl.when(z_held(d, s))
             def _():
                 products(chip(z - sign_of(s) * d, x), jnp.bitwise_xor(c, e))
 
+    def half_step_x(d, e):
         @pl.loop(0, 2)
         def _(s):
             @pl.when(x_held(d - 1, s, e))
@@ -307,7 +357,7 @@
                 def _(cc):
                     products(here, cc)
 
-            half_step(d, e)
+            half_step_z(d, e)
 
             @pl.when(e == 0)
             def _():
@@ -324,6 +374,8 @@
                             e_copy(s).start()
 
                         products(chip(s * end, y), o)
+
+            half_step_x(d, e)
 
     rows_copy.wait_recv()
     group = jnp.concatenate([rows2[0, 0:1, :n], rows2[1, 0:1, :n]], axis=1)
@@ -336,30 +388,17 @@
     prior = jnp.sum(jnp.where(diag, jnp.broadcast_to(prior_ref[...], (kh, k)), 0.0), axis=1, keepdims=True)
     psum[...] = jnp.log(prior) - 0.5 * norm
 
-    rows = 16
+    rows = 8
 
     def score_rows(i, top):
         span = pl.ds(pl.multiple_of(i * rows, rows), rows)
         re, im = pl.ds(0, n2), pl.ds(n2, n2)
-        a = {0: cres[0, span, re], HALF: cres[HALF, span, re]}
-        b = {}
-        for r in range(1, HALF):
-            a[r] = cres[r, span, re] + cres[ROT - r, span, re]
-            b[r] = cres[r, span, im] - cres[ROT - r, span, im]
-        cosine = half_transform(a, True)
-        sine = half_transform(b, False)
-        add = psum[span, :]
-        for j in range(NC):
-            base = cosine[j] + add
-            if j in (0, HALF):
-                sbuf[j, span, :] = base
-                top = jnp.maximum(top, base)
-            else:
-                low, high = base - sine[j], base + sine[j]
-                sbuf[j, span, :] = low
-                sbuf[ROT - j, span, :] = high
-                top = jnp.maximum(top, jnp.maximum(low, high))
-        return top
+        corr = turns(lambda r: cres[r, span, re], lambda r: cres[r, span, im])
+        best = None
+        for j in range(ROT):
+            sbuf[j, span, :] = corr[j]
+            best = corr[j] if best is None else jnp.maximum(best, corr[j])
+        return jnp.maximum(top, best + psum[span, :])
 
     top = lax.fori_loop(0, kh // rows, score_rows, jnp.full((rows, n2), -jnp.inf, F32))
     top = jnp.max(top, axis=0, keepdims=True)
@@ -367,8 +406,9 @@
     def exp_rows(i, total):
         span = pl.ds(pl.multiple_of(i * rows, rows), rows)
         part_sum = None
+        shift = psum[span, :] - top
         for j in range(ROT):
-            value = jnp.exp(sbuf[j, span, :] - top)
+            value = jnp.exp(sbuf[j, span, :] + shift)
             sbuf[j, span, :] = value
             part_sum = value if part_sum is None else part_sum + value
         psum[span, :] = part_sum
@@ -380,6 +420,16 @@
     stat[...] = jnp.where(which == 0, top, total)
     stat_copy = remote(stat, stat_got, ssend, srecv, sibling)
     stat_copy.start()
+
+    @pl.loop(0, kh // rows)
+    def _(i):
+        span = pl.ds(pl.multiple_of(i * rows, rows), rows)
+        real, imag = harmonics(lambda j: sbuf[j, span, :])
+        for r in range(NC):
+            sbuf[r, span, :] = real[r]
+        for r in range(1, HALF):
+            sbuf[HALF + r, span, :] = imag[r]
+
     stat_copy.wait_recv()
     other_top, other_total = stat_got[0:1, :], stat_got[1:2, :]
     most = jnp.maximum(top, other_top)
@@ -389,23 +439,19 @@
     ev_ref[...] = jnp.where(c == 0, evidence[:, :n], evidence[:, n:])
     scale = shrink / whole
 
-    @pl.loop(0, kh // rows)
+    tile = 16
+
+    @pl.loop(0, kh // tile)
     def _(i):
-        span = pl.ds(pl.multiple_of(i * rows, rows), rows)
-        u = {0: sbuf[0, span, :] * scale, HALF: sbuf[HALF, span, :] * scale}
-        v = {}
-        for j in range(1, HALF):
-            low, high = sbuf[j, span, :], sbuf[ROT - j, span, :]
-            u[j] = (low + high) * scale
-            v[j] = (low - high) * scale
-        real = half_transform(u, True)
-        imag = half_transform(v, False)
+        span = pl.ds(pl.multiple_of(i * tile, tile), tile)
         for r in range(NC):
-            re = real[r].astype(BF16)
-            im = imag[r].astype(BF16)
+            re = (sbuf[r, span, :] * scale).astype(BF16)
             pp[r, span, 0:n2] = re
-            pp[r, span, n2:] = -im
-            if 0 < r < HALF:
+            if r in (0, HALF):
+                pp[r, span, n2:] = jnp.zeros_like(re)
+            else:
+                im = (sbuf[HALF + r, span, :] * scale).astype(BF16)
+                pp[r, span, n2:] = -im
                 pp[ROT - r, span, 0:n2] = re
                 pp[ROT - r, span, n2:] = im
 
@@ -442,7 +488,7 @@
 
         @pl.loop(0, 4)
         def _(j):
-            e, s = j // 2, j % 2
+            e, s = 1 - j // 2, j % 2
 
             @pl.when(x_goes(d, s, e))
             def _():
@@ -568,29 +614,6 @@
     for i in range(mb):
         acc[c, i] = numer(here, c, i)
 
-    @pl.loop(1, dp)
-    def _(g):
-        mass_wait(g).wait_recv()
-
-    denom = 1.0 + lax.dot_general(
-        mslots[...].reshape(dp * window, k), table[...], (((0,), (0,)), ((), ())),
-        preferred_element_type=F32, precision=HIGHEST,
-    )
-    inv_ref[...] = (1.0 / denom).reshape(inv_ref.shape)
-    sib_copy.wait_recv()
-
-    for h in range(2):
-        remote(xlast.at[0], finx.at[h], rx_s.at[slot(0, 0, 0)], fx_r.at[h], sibling).wait_recv()
-        acc[h] += finx[h].astype(F32)
-    for s in range(2):
-        @pl.when(inside(z - sign_of(s)))
-        def _():
-            for h in range(2):
-                remote(xlast.at[0], finz.at[s, h], rx_s.at[slot(0, 0, 0)], fz_r.at[s, h], sibling).wait_recv()
-                acc[h] += finz[s, h].astype(F32)
-    for h in range(2):
-        out_ref[:, h] = acc[h]
-
     for e in range(2):
         for s in range(2):
             @pl.when(inside(z + sign_of(s)))
@@ -627,33 +650,73 @@
             def _():
                 x_sum(d, s, e).wait_send()
 
-            @pl.when(inside(z + sign_of(s) * d))
-            def _():
-                z_got(d, s, e).wait_send()
-
     for s in range(2):
         @pl.when(inside(z + sign_of(s)))
         def _():
             e_copy(s).wait_send()
             e_sum(s).wait_send()
-    for e in range(2):
-        x_last(e).wait_send()
 
     @pl.loop(1, dp)
     def _(g):
         mass_copy(g).wait_send()
 
-
-def finish_kernel(total_ref, inv_ref, ev_ref, out_ref, evidence_ref, buf, sems):
-    copies = []
-    for i in range(total_ref.shape[0]):
-        buf[i] = total_ref[i] * inv_ref[...]
-        copy = pltpu.make_async_copy(buf.at[i], out_ref.at[i], sems.at[i])
-        copy.start()
-        copies.append(copy)
+    @pl.loop(1, dp)
+    def _(g):
+        mass_wait(g).wait_recv()
+
+    denom = 1.0 + lax.dot_general(
+        mslots[...].reshape(dp * window, k), table[...], (((0,), (0,)), ((), ())),
+        preferred_element_type=F32, precision=HIGHEST,
+    )
+    inv[...] = (1.0 / denom).reshape(inv.shape)
+    sib_copy.wait_recv()
+
+    def got_x(h):
+        remote(xlast.at[0], finx.at[h], rx_s.at[slot(0, 0, 0)], fx_r.at[h], sibling).wait_recv()
+
+    def got_z(s, h):
+        remote(xlast.at[0], finz.at[s, h], rx_s.at[slot(0, 0, 0)], fz_r.at[s, h], sibling).wait_recv()
+
+    for h in range(2):
+        got_z(near, h)
+        for i in range(mb):
+            acc[h, i] += finz[near, h, i].astype(F32)
+    for h in range(2):
+        got_x(h)
+
+    @pl.when(is_end(z))
+    def _():
+        for h in range(2):
+            for i in range(mb):
+                out_ref[i, h] = (acc[h, i] + finx[h, i].astype(F32)) * inv[h]
+
+    @pl.when(jnp.logical_not(is_end(z)))
+    def _():
+        for h in range(2):
+            got_z(1 - near, h)
+            for i in range(mb):
+                total = acc[h, i] + finx[h, i].astype(F32)
+                out_ref[i, h] = (total + finz[1 - near, h, i].astype(F32)) * inv[h]
+
+    @pl.loop(1, zn)
+    def _(d):
+        @pl.loop(0, 4)
+        def _(j):
+            e, s = j // 2, j % 2
+
+            @pl.when(inside(z + sign_of(s) * d))
+            def _():
+                z_got(d, s, e).wait_send()
+
+    for e in range(2):
+        x_last(e).wait_send()
+
+
+def finish_kernel(total_ref, ev_ref, out_ref, evidence_ref, sem):
+    copy = pltpu.make_async_copy(total_ref, out_ref, sem)
+    copy.start()
     evidence_ref[...] = ev_ref[...]
-    for copy in copies:
-        copy.wait()
+    copy.wait()
 
 
 def shards(dp, particles, refs, ctf_group, defocus, class_prior, cycle_weight):
@@ -670,16 +733,16 @@
     vmem = pl.BlockSpec(memory_space=pltpu.VMEM)
     hbm = pl.BlockSpec(memory_space=pl.ANY)
     sem = pltpu.SemaphoreType.DMA
-    total, inv, ev = pl.pallas_call(
+    total, ev = pl.pallas_call(
         functools.partial(step_kernel, zn, dp, window),
         out_shape=(
             jax.ShapeDtypeStruct((mb, 2, kh, q), F32),
-            jax.ShapeDtypeStruct((2, kh, q), F32),
             jax.ShapeDtypeStruct((1, n), F32),
         ),
         in_specs=[pl.BlockSpec(memory_space=pltpu.MemorySpace.HBM)] * 6,
-        out_specs=(vmem, vmem, vmem),
+        out_specs=(vmem, vmem),
         scratch_shapes=[
+            pltpu.VMEM((2, kh, q), F32),
             pltpu.VMEM((1, n), jnp.int32), pltpu.VMEM((1, G), F32),
             pltpu.VMEM((1, R), F32), pltpu.VMEM((1, k), F32), sem((4,)),
             pltpu.VMEM((n, m_all, q), BF16),
@@ -730,12 +793,12 @@
             jax.ShapeDtypeStruct((mb, 2, kh, q), F32),
             jax.ShapeDtypeStruct((1, n), F32),
         ),
-        in_specs=[vmem] * 3,
+        in_specs=[vmem] * 2,
         out_specs=(hbm, vmem),
-        scratch_shapes=[pltpu.VMEM((mb, 2, kh, q), F32), sem((mb,))],
+        scratch_shapes=[sem],
         compiler_params=pltpu.CompilerParams(vmem_limit_bytes=8 << 20),
         name="finish",
-    )(total, inv, ev)
+    )(total, ev)
     return (new_refs.reshape(mb, k, q), evidence[0])
 
 

time: 59.1 us -> 58.1 us (0.983)
  Pallas kernels: 58.3 us -> 57.3 us
    pallas_call x1, Pallas kernels: 57 us -> 56 us  [shards(): pl.pallas_call(functools.partial(step_kernel, zn, dp, window), out_shape=...]
where the time goes in v4:
time: 58.1 us; the launch traced here: 57.9 us
  Pallas kernels  57.3 us (99%)
  between operations  0.64 us (1%)
    pallas_call x1, Pallas kernels, shards(): pl.pallas_call(functools.partial(step_kernel, zn, dp, window), out_shape=...  56 us
    pallas_call x1, Pallas kernels, shards(): pl.pallas_call(finish_kernel, out_shape=(jax.ShapeDtypeStruct((mb, 2, kh,...  1.31 us

profile of v4, /device:TPU:0, one launch (start us, length us, event | category | flops | bytes accessed | tf_op | source)
XLA Modules:
  0.0 57.9 jit_solution(10808323620255796653)
XLA Ops:
  0.6 56.0 %step.1 = (f32[8,2,64,128]{3,2,1,0:T(8,128)S(1)}, f32[1,64]{1,0:T(1,128)S(1)}) custom-call(bf16[8,2,64,128]{3,2,1,0:T(8,128)(2,1)} %bitcast.7, bf16[64,128,128]{2,1,0:T(8,128)(2,1)} %refs_1_.1, s32[1,64]{1,0:T(1,128)} %bitcast.8, f32[1,32]{1,0:T(1,128)} %bitcast.9, f32[1,64]{1,0:T(1,128)} %bitcast.10, f32[1,128]{1,0:T(1,128)} %bitcast.11), custom_call_target="tpu_custom_call" | custom-call | tf_op jit(solution)/shard_map/step/pallas_call | solution.py:736
  56.6 1.3 %finish.1 = (f32[8,2,64,128]{3,2,1,0:T(8,128)}, f32[1,64]{1,0:T(1,128)}) custom-call(f32[8,2,64,128]{3,2,1,0:T(8,128)S(1)} %get-tuple-element.6.total_ref, f32[1,64]{1,0:T(1,128)S(1)} %get-tuple-element.7.ev_ref), custom_call_target="tpu_custom_call" | custom-call | tf_op jit(solution)/shard_map/finish/pallas_call | solution.py:790

commit v5 on v4

--- a/solution.py
+++ b/solution.py
@@ -155,6 +155,16 @@
 
     sibling = at(z, x, o)
 
+    def each(low, high, body):
+        if high - low <= 8:
+            for value in range(low, high):
+                body(value)
+        else:
+            pl.loop(low, high)(body)
+
+    def fixed(d, value):
+        return isinstance(d, int) and d == value
+
     barrier = pltpu.get_barrier_semaphore()
 
     def greet(target):
@@ -182,6 +192,31 @@
     mine = pltpu.make_async_copy(refs_ref.at[:, c], held.at[chip(z, x), c], keep)
     mine.start()
 
+    pl.semaphore_wait(
+        barrier, 3 + 2 * (z > 0).astype(jnp.int32) + 2 * (z < end).astype(jnp.int32)
+    )
+
+    here = chip(z, x)
+
+    def first_z(s, e):
+        cc = jnp.bitwise_xor(c, e)
+        return remote(refs_ref.at[:, cc], held.at[here, c], az_s.at[slot(0, s, e)],
+                      az_r.at[slot(1, s, e)], at(z + sign_of(s), x, cc))
+
+    def first_x(e):
+        cc = jnp.bitwise_xor(c, e)
+        return remote(refs_ref.at[:, cc], held.at[here, c], ax_s.at[slot(0, 0, e)],
+                      ax_r.at[slot(0, 0, e)], at(z, y, cc))
+
+    for e in range(2):
+        for s in range(2):
+            @pl.when(inside(z + sign_of(s)))
+            def _():
+                first_z(s, e).start()
+        first_x(1 - e).start()
+    own_half = remote(refs_ref.at[:, o], held.at[here, c], ksend, krecv, sibling)
+    own_half.start()
+
     for copy in smalls:
         copy.wait()
     lane = lax.broadcasted_iota(jnp.int32, (G, q), 1)
@@ -201,31 +236,6 @@
     )
     row = row_ref[...].astype(F32)
     rows2[c] = jnp.broadcast_to(jnp.concatenate([row, row], axis=1), rows2.shape[1:])
-
-    pl.semaphore_wait(
-        barrier, 3 + 2 * (z > 0).astype(jnp.int32) + 2 * (z < end).astype(jnp.int32)
-    )
-
-    here = chip(z, x)
-
-    def first_z(s, e):
-        cc = jnp.bitwise_xor(c, e)
-        return remote(refs_ref.at[:, cc], held.at[here, c], az_s.at[slot(0, s, e)],
-                      az_r.at[slot(1, s, e)], at(z + sign_of(s), x, cc))
-
-    def first_x(e):
-        cc = jnp.bitwise_xor(c, e)
-        return remote(refs_ref.at[:, cc], held.at[here, c], ax_s.at[slot(0, 0, e)],
-                      ax_r.at[slot(0, 0, e)], at(z, y, cc))
-
-    for e in range(2):
-        for s in range(2):
-            @pl.when(inside(z + sign_of(s)))
-            def _():
-                first_z(s, e).start()
-        first_x(e).start()
-    own_half = remote(refs_ref.at[:, o], held.at[here, c], ksend, krecv, sibling)
-    own_half.start()
     rows_copy = remote(rows2.at[c], rows2.at[c], rsend, rrecv, sibling)
     rows_copy.start()
 
@@ -301,6 +311,8 @@
 
     def x_held(d, s, e):
         far = jnp.logical_and(inside(z - sign_of(s) * d), by_x(z - sign_of(s) * d, e))
+        if isinstance(d, int):
+            return far
         return jnp.logical_or(jnp.logical_and(d > 0, far), jnp.logical_and(d == 0, s == 0))
 
     def z_forward(d, s, e):
@@ -308,74 +320,144 @@
         def _():
             z_wait(d, s, e).wait_recv()
 
-            @pl.when(inside(z + sign_of(s)))
-            def _():
-                z_copy(d, s, e).start()
-
-            @pl.when(by_x(z - sign_of(s) * d, e))
-            def _():
-                x_copy(d, s, e).start()
-
-    def half_step_z(d, e):
+            if not fixed(d, end):
+                @pl.when(inside(z + sign_of(s)))
+                def _():
+                    z_copy(d, s, e).start()
+
+            if not (fixed(d, end) and e == 1):
+                @pl.when(by_x(z - sign_of(s) * d, e))
+                def _():
+                    x_copy(d, s, e).start()
+
+    def x_take(d, s, e):
+        x_wait(d - 1, s, e).wait_recv()
+        for t in range(2):
+            if e == 1 and (not isinstance(d, int) or d == 1):
+                @pl.when(z == t * end if isinstance(d, int) else jnp.logical_and(d == 1, z == t * end))
+                def _():
+                    e_copy(t).start()
+
+        products(chip(z - sign_of(s) * (d - 1), y), jnp.bitwise_xor(c, e))
+
+    def e_take(d, s):
+        gone = z if s == 0 else end - z
+
+        @pl.when(jnp.logical_and(gone == d - 1, gone > 0))
+        def _():
+            e_copy(s).wait_recv()
+
+            if not fixed(d, zn):
+                @pl.when(gone < end)
+                def _():
+                    e_copy(s).start()
+
+            products(chip(s * end, y), o)
+
+    def opening():
+        @pl.loop(0, m_all // chunk)
+        def _(i):
+            weighted_copy(i).wait_recv()
+
+        own_half.wait_recv()
+
         @pl.loop(0, 2)
-        def _(s):
+        def _(cc):
+            products(here, cc)
+
+    mine.wait()
+
+    def gather_step(d):
+        for e in range(2):
+            if not fixed(d, zn):
+                for s in range(2):
+                    z_forward(d, s, e)
+
+            if e == 0:
+                if isinstance(d, int):
+                    if d == 1:
+                        opening()
+                else:
+                    pl.when(d == 1)(opening)
+
+            if not fixed(d, zn):
+                for s in range(2):
+                    @pl.when(z_held(d, s))
+                    def _():
+                        products(chip(z - sign_of(s) * d, x), jnp.bitwise_xor(c, e))
+
+            if e == 0 and not fixed(d, 1):
+                for s in range(2):
+                    e_take(d, s)
+
+            if fixed(d, 1):
+                x_take(d, 0, e)
+            elif not (fixed(d, zn) and e == 1):
+                for s in range(2):
+                    @pl.when(x_held(d - 1, s, e))
+                    def _():
+                        x_take(d, s, e)
+
+    def x_arrive(e):
+        x_wait(0, 0, e).wait_recv()
+        if e == 1:
+            for t in range(2):
+                @pl.when(z == t * end)
+                def _():
+                    e_copy(t).start()
+
+    def z_products(d, e):
+        for s in range(2):
             @pl.when(z_held(d, s))
             def _():
                 products(chip(z - sign_of(s) * d, x), jnp.bitwise_xor(c, e))
 
-    def half_step_x(d, e):
-        @pl.loop(0, 2)
-        def _(s):
-            @pl.when(x_held(d - 1, s, e))
-            def _():
-                x_wait(d - 1, s, e).wait_recv()
-                for t in range(2):
-                    @pl.when(jnp.logical_and(jnp.logical_and(d == 1, e == 1), z == t * end))
+    def e_taken(s, d):
+        gone = z if s == 0 else end - z
+        return jnp.logical_and(gone == d - 1, gone > 0)
+
+    def gather_fixed(d):
+        if d < zn:
+            for s in range(2):
+                z_forward(d, s, 0)
+        if d == 1:
+            x_arrive(1)
+            opening()
+        else:
+            for s in range(2):
+                @pl.when(e_taken(s, d))
+                def _():
+                    e_copy(s).wait_recv()
+                    if d < zn:
+                        e_copy(s).start()
+        if d < zn:
+            z_products(d, 0)
+        if d > 1:
+            for s in range(2):
+                @pl.when(e_taken(s, d))
+                def _():
+                    products(chip(s * end, y), o)
+        if d < zn:
+            for s in range(2):
+                z_forward(d, s, 1)
+        if d == 1:
+            x_arrive(0)
+        for e in range(2):
+            if e == 1 and d < zn:
+                z_products(d, 1)
+            if d == 1:
+                products(chip(z, y), jnp.bitwise_xor(c, 1 - e))
+            elif not (d == zn and e == 1):
+                for s in range(2):
+                    @pl.when(x_held(d - 1, s, e))
                     def _():
-                        e_copy(t).start()
-
-                products(chip(z - sign_of(s) * (d - 1), y), jnp.bitwise_xor(c, e))
-
-    mine.wait()
-
-    @pl.loop(1, zn + 1)
-    def _(d):
-        @pl.loop(0, 2)
-        def _(e):
-            for s in range(2):
-                z_forward(d, s, e)
-
-            @pl.when(jnp.logical_and(d == 1, e == 0))
-            def _():
-                @pl.loop(0, m_all // chunk)
-                def _(i):
-                    weighted_copy(i).wait_recv()
-
-                own_half.wait_recv()
-
-                @pl.loop(0, 2)
-                def _(cc):
-                    products(here, cc)
-
-            half_step_z(d, e)
-
-            @pl.when(e == 0)
-            def _():
-                @pl.loop(0, 2)
-                def _(s):
-                    gone = jnp.where(s == 0, z, end - z)
-
-                    @pl.when(jnp.logical_and(gone == d - 1, gone > 0))
-                    def _():
-                        e_copy(s).wait_recv()
-
-                        @pl.when(gone < end)
-                        def _():
-                            e_copy(s).start()
-
-                        products(chip(s * end, y), o)
-
-            half_step_x(d, e)
+                        x_take(d, s, e)
+
+    if zn <= 8:
+        for d in range(1, zn + 1):
+            gather_fixed(d)
+    else:
+        each(1, zn + 1, gather_step)
 
     rows_copy.wait_recv()
     group = jnp.concatenate([rows2[0, 0:1, :n], rows2[1, 0:1, :n]], axis=1)
@@ -482,21 +564,22 @@
         zo = z + sign_of(s) * d
         return jnp.logical_and(inside(zo), by_x(zo, e))
 
-    @pl.loop(0, zn - 1)
-    def _(t):
+    def x_step(t):
         d = end - t
-
-        @pl.loop(0, 4)
-        def _(j):
-            e, s = 1 - j // 2, j % 2
-
-            @pl.when(x_goes(d, s, e))
-            def _():
-                for i in range(mb):
-                    xsend[slot(d, s, e), i] = numer(
-                        chip(z + sign_of(s) * d, y), jnp.bitwise_xor(c, e), i
-                    ).astype(BF16)
-                x_sum(d, s, e).start()
+        for e in (1, 0):
+            for s in range(2):
+                if fixed(d, end) and e == 1:
+                    continue
+
+                @pl.when(x_goes(d, s, e))
+                def _():
+                    for i in range(mb):
+                        xsend[slot(d, s, e), i] = numer(
+                            chip(z + sign_of(s) * d, y), jnp.bitwise_xor(c, e), i
+                        ).astype(BF16)
+                    x_sum(d, s, e).start()
+
+    each(0, zn - 1, x_step)
 
     def send_last(e, extra):
         for i in range(mb):
@@ -512,34 +595,6 @@
         def _():
             send_last(e, None)
 
-    start = (here * n2 * G) // nall
-    hot = (
-        group == (lax.broadcasted_iota(jnp.int32, (window, n2), 0) + start).astype(F32)
-    ).astype(F32)
-    part_mass = lax.dot_general(
-        hot, psum[...] * scale, (((1,), (1,)), ((), ())), preferred_element_type=F32, precision=HIGHEST,
-    )
-    nothing = jnp.zeros_like(part_mass)
-    mass[...] = jnp.where(
-        c == 0, jnp.concatenate([part_mass, nothing], axis=1), jnp.concatenate([nothing, part_mass], axis=1)
-    )
-    mslots[me] = mass[...]
-
-    def mass_copy(g):
-        return remote(mass, mslots.at[me], msend.at[g], mrecv.at[g], lax.rem(me + g, dp))
-
-    def mass_wait(g):
-        return remote(mass, mslots.at[lax.rem(me + dp - g, dp)], msend.at[g], mrecv.at[g], sibling)
-
-    @pl.loop(1, dp)
-    def _(g):
-        mass_copy(g).start()
-
-    for i in range(mb):
-        sib[i] = numer(here, o, i)
-    sib_copy = remote(sib, acc.at[c], bsend, brecv, sibling)
-    sib_copy.start()
-
     def z_sum(d, s, e):
         return remote(zsend.at[slot(d, s, e)], zrecv.at[slot(d - 1, s, e)],
                       rz_s.at[slot(d, s, e)], rz_r.at[slot(d - 1, s, e)], at(z + sign_of(s), x, c))
@@ -554,28 +609,28 @@
 
     near = (2 * z < zn).astype(jnp.int32)
 
-    @pl.loop(0, zn - 1)
-    def _(t):
-        d = end - t
-
+    def e_pass(d):
         for s in range(2):
             left = (end - z) if s == 0 else z
 
-            @pl.when(jnp.logical_and(left == d, left < end))
+            @pl.when(jnp.logical_and(left == d - 1, jnp.logical_and(left > 0, left < end)))
             def _():
                 e_sum(s).wait_recv()
                 for i in range(mb):
                     esend[s, i] = (numer(chip(end - s * end, y), o, i) + erecv[s, i].astype(F32)).astype(BF16)
                 e_sum(s).start()
 
+    def e_cross():
         for s in range(2):
-            @pl.when(jnp.logical_and(d == 1, z == (1 - s) * end))
+            @pl.when(z == (1 - s) * end)
             def _():
                 e_sum(s).wait_recv()
                 send_last(1, s)
 
-        @pl.loop(0, 4)
-        def _(j):
+    def z_step(t, between=None):
+        d = end - t
+
+        def part(j):
             e = 1 - j // 2
             s = jnp.bitwise_xor(j % 2, near)
             zo = z + sign_of(s) * d
@@ -603,13 +658,64 @@
                 for i in range(mb):
                     zsend[here_slot, i] = acc[c, i].astype(BF16)
 
-                @pl.when(d > 1)
-                def _():
-                    z_sum(d, s, e).start()
-
-                @pl.when(d == 1)
-                def _():
-                    z_last(s, e).start()
+                if isinstance(d, int):
+                    (z_sum(d, s, e) if d > 1 else z_last(s, e)).start()
+                else:
+                    @pl.when(d > 1)
+                    def _():
+                        z_sum(d, s, e).start()
+
+                    @pl.when(d == 1)
+                    def _():
+                        z_last(s, e).start()
+
+        for j in range(2):
+            part(j)
+        if between is not None:
+            between()
+        if isinstance(d, int):
+            if d == 1:
+                e_cross()
+            else:
+                e_pass(d)
+        else:
+            pl.when(d == 1)(e_cross)
+            e_pass(d)
+        for j in range(2, 4):
+            part(j)
+
+    def mass_copy(g):
+        return remote(mass, mslots.at[me], msend.at[g], mrecv.at[g], lax.rem(me + g, dp))
+
+    def mass_wait(g):
+        return remote(mass, mslots.at[lax.rem(me + dp - g, dp)], msend.at[g], mrecv.at[g], sibling)
+
+    sib_copy = remote(sib, acc.at[c], bsend, brecv, sibling)
+
+    def side_work():
+        start = (here * n2 * G) // nall
+        hot = (
+            group == (lax.broadcasted_iota(jnp.int32, (window, n2), 0) + start).astype(F32)
+        ).astype(F32)
+        part_mass = lax.dot_general(
+            hot, psum[...] * scale, (((1,), (1,)), ((), ())), preferred_element_type=F32, precision=HIGHEST,
+        )
+        nothing = jnp.zeros_like(part_mass)
+        mass[...] = jnp.where(
+            c == 0, jnp.concatenate([part_mass, nothing], axis=1), jnp.concatenate([nothing, part_mass], axis=1)
+        )
+        mslots[me] = mass[...]
+
+        @pl.loop(1, dp)
+        def _(g):
+            mass_copy(g).start()
+
+        for i in range(mb):
+            sib[i] = numer(here, o, i)
+        sib_copy.start()
+
+    z_step(0, side_work)
+    each(1, zn - 1, z_step)
 
     for i in range(mb):
         acc[c, i] = numer(here, c, i)
@@ -698,25 +804,29 @@
                 total = acc[h, i] + finx[h, i].astype(F32)
                 out_ref[i, h] = (total + finz[1 - near, h, i].astype(F32)) * inv[h]
 
-    @pl.loop(1, zn)
-    def _(d):
-        @pl.loop(0, 4)
-        def _(j):
-            e, s = j // 2, j % 2
-
+    def sums_sent(d):
+        for s in range(2):
             @pl.when(inside(z + sign_of(s) * d))
             def _():
-                z_got(d, s, e).wait_send()
+                for e in range(2):
+                    z_got(d, s, e).wait_send()
+
+    each(1, zn, sums_sent)
 
     for e in range(2):
         x_last(e).wait_send()
 
 
-def finish_kernel(total_ref, ev_ref, out_ref, evidence_ref, sem):
-    copy = pltpu.make_async_copy(total_ref, out_ref, sem)
-    copy.start()
+def finish_kernel(total_ref, ev_ref, out_ref, evidence_ref, sems):
+    copies = [
+        pltpu.make_async_copy(total_ref.at[i], out_ref.at[i], sems.at[i])
+        for i in range(total_ref.shape[0])
+    ]
+    for copy in copies:
+        copy.start()
     evidence_ref[...] = ev_ref[...]
-    copy.wait()
+    for copy in copies:
+        copy.wait()
 
 
 def shards(dp, particles, refs, ctf_group, defocus, class_prior, cycle_weight):
@@ -795,7 +905,7 @@
         ),
         in_specs=[vmem] * 2,
         out_specs=(hbm, vmem),
-        scratch_shapes=[sem],
+        scratch_shapes=[sem((mb,))],
         compiler_params=pltpu.CompilerParams(vmem_limit_bytes=8 << 20),
         name="finish",
     )(total, ev)

time: 58.1 us -> 56.4 us (0.971)
  Pallas kernels: 57.3 us -> 55.4 us
    pallas_call x1, Pallas kernels: 56 us -> 54.1 us  [shards(): pl.pallas_call(functools.partial(step_kernel, zn, dp, window), out_shape=...]
where the time goes in v5:
time: 56.4 us; the launch traced here: 56.2 us
  Pallas kernels  55.4 us (98%)
  between operations  0.8 us (1%)
    pallas_call x1, Pallas kernels, shards(): pl.pallas_call(functools.partial(step_kernel, zn, dp, window), out_shape=...  54.1 us
    pallas_call x1, Pallas kernels, shards(): pl.pallas_call(finish_kernel, out_shape=(jax.ShapeDtypeStruct((mb, 2, kh,...  1.36 us

profile of v5, /device:TPU:0, one launch (start us, length us, event | category | flops | bytes accessed | tf_op | source)
XLA Modules:
  0.0 56.2 jit_solution(15007774466231723487)
XLA Ops:
  0.6 54.1 %step.1 = (f32[8,2,64,128]{3,2,1,0:T(8,128)S(1)}, f32[1,64]{1,0:T(1,128)S(1)}) custom-call(bf16[8,2,64,128]{3,2,1,0:T(8,128)(2,1)} %bitcast.7, bf16[64,128,128]{2,1,0:T(8,128)(2,1)} %refs_1_.1, s32[1,64]{1,0:T(1,128)} %bitcast.8, f32[1,32]{1,0:T(1,128)} %bitcast.9, f32[1,64]{1,0:T(1,128)} %bitcast.10, f32[1,128]{1,0:T(1,128)} %bitcast.11), custom_call_target="tpu_custom_call" | custom-call | tf_op jit(solution)/shard_map/step/pallas_call | solution.py:846
  54.7 1.4 %finish.1 = (f32[8,2,64,128]{3,2,1,0:T(8,128)}, f32[1,64]{1,0:T(1,128)}) custom-call(f32[8,2,64,128]{3,2,1,0:T(8,128)S(1)} %get-tuple-element.6.total_ref, f32[1,64]{1,0:T(1,128)S(1)} %get-tuple-element.7.ev_ref), custom_call_target="tpu_custom_call" | custom-call | tf_op jit(solution)/shard_map/finish/pallas_call | solution.py:900

commit v6 on v5

--- a/solution.py
+++ b/solution.py
@@ -112,7 +112,7 @@
     (refs_ref, part_ref, row_hbm, focus_hbm, cw_hbm, prior_hbm,
      out_ref, ev_ref,
      inv, row_ref, focus_ref, cw_ref, prior_ref, small, part, both, held, cres, energy, sbuf, psum, pp, rows2, table,
-     stat, stat_got, mass, mslots,
+     stat, stat_got, halves, mass, mslots,
      xsend, xrecv, zsend, zrecv, xlast, esend, erecv, sib, acc, finx, finz,
      psem, keep, ksend, krecv, wsend, wrecv, rsend, rrecv,
      ax_s, ax_r, az_s, az_r, ae_s, ae_r, ssend, srecv, msend, mrecv,
@@ -262,8 +262,7 @@
     for p in range(dp // 2):
         pick = (below == -((p * n2 * G) // nall)).astype(F32)
         span = jnp.dot(pick, power, precision=HIGHEST, preferred_element_type=F32)
-        table[2 * p * window:(2 * p + 1) * window, :] = span
-        table[(2 * p + 1) * window:(2 * p + 2) * window, :] = span
+        table[p * window:(p + 1) * window, :] = span
 
     def products(block, cc):
         total = None
@@ -545,6 +544,34 @@
     def e_sum(s):
         return remote(esend.at[s], erecv.at[s], re_s.at[s], re_r.at[s], at(z + sign_of(s), x, c))
 
+    def x_sum(d, s, e):
+        return remote(xsend.at[slot(d, s, e)], xrecv.at[slot(d, s, e)],
+                      rx_s.at[slot(d, s, e)], rx_r.at[slot(d, s, e)], at(z, y, c))
+
+    def x_last(e):
+        return remote(xlast.at[e], finx.at[c], rx_s.at[slot(0, 0, e)], fx_r.at[c],
+                      at(z, y, jnp.bitwise_xor(c, e)))
+
+    def x_goes(d, s, e):
+        zo = z + sign_of(s) * d
+        return jnp.logical_and(inside(zo), by_x(zo, e))
+
+    def x_step(t):
+        d = end - t
+        for e in (1, 0):
+            for s in range(2):
+                if fixed(d, end) and e == 1:
+                    continue
+
+                @pl.when(x_goes(d, s, e))
+                def _():
+                    for i in range(mb):
+                        xsend[slot(d, s, e), i] = numer(
+                            chip(z + sign_of(s) * d, y), jnp.bitwise_xor(c, e), i
+                        ).astype(BF16)
+                    x_sum(d, s, e).start()
+
+    x_step(0)
     for s in range(2):
         @pl.when(z == s * end)
         def _():
@@ -552,34 +579,7 @@
                 esend[s, i] = numer(chip(end - s * end, y), o, i).astype(BF16)
             e_sum(s).start()
 
-    def x_sum(d, s, e):
-        return remote(xsend.at[slot(d, s, e)], xrecv.at[slot(d, s, e)],
-                      rx_s.at[slot(d, s, e)], rx_r.at[slot(d, s, e)], at(z, y, c))
-
-    def x_last(e):
-        return remote(xlast.at[e], finx.at[c], rx_s.at[slot(0, 0, e)], fx_r.at[c],
-                      at(z, y, jnp.bitwise_xor(c, e)))
-
-    def x_goes(d, s, e):
-        zo = z + sign_of(s) * d
-        return jnp.logical_and(inside(zo), by_x(zo, e))
-
-    def x_step(t):
-        d = end - t
-        for e in (1, 0):
-            for s in range(2):
-                if fixed(d, end) and e == 1:
-                    continue
-
-                @pl.when(x_goes(d, s, e))
-                def _():
-                    for i in range(mb):
-                        xsend[slot(d, s, e), i] = numer(
-                            chip(z + sign_of(s) * d, y), jnp.bitwise_xor(c, e), i
-                        ).astype(BF16)
-                    x_sum(d, s, e).start()
-
-    each(0, zn - 1, x_step)
+    each(1, zn - 1, x_step)
 
     def send_last(e, extra):
         for i in range(mb):
@@ -653,10 +653,12 @@
                 def _():
                     z_got(d, s, e).wait_recv()
                     for i in range(mb):
-                        acc[c, i] += zrecv[here_slot, i].astype(F32)
-
-                for i in range(mb):
-                    zsend[here_slot, i] = acc[c, i].astype(BF16)
+                        zsend[here_slot, i] = (acc[c, i] + zrecv[here_slot, i].astype(F32)).astype(BF16)
+
+                @pl.when(jnp.logical_not(line))
+                def _():
+                    for i in range(mb):
+                        zsend[here_slot, i] = acc[c, i].astype(BF16)
 
                 if isinstance(d, int):
                     (z_sum(d, s, e) if d > 1 else z_last(s, e)).start()
@@ -684,12 +686,15 @@
         for j in range(2, 4):
             part(j)
 
+    chips = dp // 2
+
     def mass_copy(g):
-        return remote(mass, mslots.at[me], msend.at[g], mrecv.at[g], lax.rem(me + g, dp))
+        return remote(mass, mslots.at[here], msend.at[g], mrecv.at[g], lax.rem(here + g, chips) * 2 + c)
 
     def mass_wait(g):
-        return remote(mass, mslots.at[lax.rem(me + dp - g, dp)], msend.at[g], mrecv.at[g], sibling)
-
+        return remote(mass, mslots.at[lax.rem(here + chips - g, chips)], msend.at[g], mrecv.at[g], sibling)
+
+    halves_copy = remote(halves.at[c], halves.at[c], msend.at[0], mrecv.at[0], sibling)
     sib_copy = remote(sib, acc.at[c], bsend, brecv, sibling)
 
     def side_work():
@@ -701,18 +706,21 @@
             hot, psum[...] * scale, (((1,), (1,)), ((), ())), preferred_element_type=F32, precision=HIGHEST,
         )
         nothing = jnp.zeros_like(part_mass)
-        mass[...] = jnp.where(
+        halves[c] = jnp.where(
             c == 0, jnp.concatenate([part_mass, nothing], axis=1), jnp.concatenate([nothing, part_mass], axis=1)
         )
-        mslots[me] = mass[...]
-
-        @pl.loop(1, dp)
-        def _(g):
-            mass_copy(g).start()
-
+        halves_copy.start()
         for i in range(mb):
             sib[i] = numer(here, o, i)
         sib_copy.start()
+        halves_copy.wait_recv()
+        both_mass = halves[0] + halves[1]
+        mass[...] = both_mass
+        mslots[here] = both_mass
+
+        @pl.loop(1, dp // 2)
+        def _(g):
+            mass_copy(g).start()
 
     z_step(0, side_work)
     each(1, zn - 1, z_step)
@@ -762,16 +770,18 @@
             e_copy(s).wait_send()
             e_sum(s).wait_send()
 
-    @pl.loop(1, dp)
+    halves_copy.wait_send()
+
+    @pl.loop(1, dp // 2)
     def _(g):
         mass_copy(g).wait_send()
 
-    @pl.loop(1, dp)
+    @pl.loop(1, dp // 2)
     def _(g):
         mass_wait(g).wait_recv()
 
     denom = 1.0 + lax.dot_general(
-        mslots[...].reshape(dp * window, k), table[...], (((0,), (0,)), ((), ())),
+        mslots[...].reshape(dp // 2 * window, k), table[...], (((0,), (0,)), ((), ())),
         preferred_element_type=F32, precision=HIGHEST,
     )
     inv[...] = (1.0 / denom).reshape(inv.shape)
@@ -817,16 +827,11 @@
         x_last(e).wait_send()
 
 
-def finish_kernel(total_ref, ev_ref, out_ref, evidence_ref, sems):
-    copies = [
-        pltpu.make_async_copy(total_ref.at[i], out_ref.at[i], sems.at[i])
-        for i in range(total_ref.shape[0])
-    ]
-    for copy in copies:
-        copy.start()
+def finish_kernel(total_ref, ev_ref, out_ref, evidence_ref, sem):
+    copy = pltpu.make_async_copy(total_ref, out_ref, sem)
+    copy.start()
     evidence_ref[...] = ev_ref[...]
-    for copy in copies:
-        copy.wait()
+    copy.wait()
 
 
 def shards(dp, particles, refs, ctf_group, defocus, class_prior, cycle_weight):
@@ -864,11 +869,12 @@
             pltpu.VMEM((kh, n2), F32),
             pltpu.VMEM((ROT, kh, 2 * n2), BF16),
             pltpu.VMEM((2, 8, n2), F32),
-            pltpu.VMEM((dp * window, q), F32),
+            pltpu.VMEM((dp // 2 * window, q), F32),
             pltpu.VMEM((8, n2), F32),
             pltpu.VMEM((8, n2), F32),
+            pltpu.VMEM((2, window, k), F32),
             pltpu.VMEM((window, k), F32),
-            pltpu.VMEM((dp, window, k), F32),
+            pltpu.VMEM((dp // 2, window, k), F32),
             pltpu.VMEM((slots, mb, kh, q), BF16),
             pltpu.VMEM((slots, mb, kh, q), BF16),
             pltpu.VMEM((slots, mb, kh, q), BF16),
@@ -882,7 +888,7 @@
             pltpu.VMEM((2, 2, mb, kh, q), BF16),
             sem, sem, sem, sem, sem((weighted_chunks,)), sem((weighted_chunks,)), sem, sem,
             sem((slots,)), sem((slots,)), sem((slots,)), sem((slots + 4,)), sem((2,)), sem((2,)),
-            sem, sem, sem((dp,)), sem((dp,)),
+            sem, sem, sem((dp // 2,)), sem((dp // 2,)),
             sem((slots,)), sem((slots,)), sem((slots,)), sem((slots,)), sem((2,)), sem((2,)),
             sem((2,)), sem((2, 2)), sem, sem,
         ],
@@ -905,7 +911,7 @@
         ),
         in_specs=[vmem] * 2,
         out_specs=(hbm, vmem),
-        scratch_shapes=[sem((mb,))],
+        scratch_shapes=[sem],
         compiler_params=pltpu.CompilerParams(vmem_limit_bytes=8 << 20),
         name="finish",
     )(total, ev)

time: 56.4 us -> 55.8 us (0.989)
  no operation moved by 1% of the time
where the time goes in v6:
time: 55.8 us; the launch traced here: 55.7 us
  Pallas kernels  54.9 us (98%)
  between operations  0.8 us (1%)
    pallas_call x1, Pallas kernels, shards(): pl.pallas_call(functools.partial(step_kernel, zn, dp, window), out_shape=...  53.6 us
    pallas_call x1, Pallas kernels, shards(): pl.pallas_call(finish_kernel, out_shape=(jax.ShapeDtypeStruct((mb, 2, kh,...  1.31 us

profile of v6, /device:TPU:0, one launch (start us, length us, event | category | flops | bytes accessed | tf_op | source)
XLA Modules:
  0.0 55.7 jit_solution(3879983758058012285)
XLA Ops:
  0.6 53.6 %step.1 = (f32[8,2,64,128]{3,2,1,0:T(8,128)S(1)}, f32[1,64]{1,0:T(1,128)S(1)}) custom-call(bf16[8,2,64,128]{3,2,1,0:T(8,128)(2,1)} %bitcast.7, bf16[64,128,128]{2,1,0:T(8,128)(2,1)} %refs_1_.1, s32[1,64]{1,0:T(1,128)} %bitcast.8, f32[1,32]{1,0:T(1,128)} %bitcast.9, f32[1,64]{1,0:T(1,128)} %bitcast.10, f32[1,128]{1,0:T(1,128)} %bitcast.11), custom_call_target="tpu_custom_call" | custom-call | tf_op jit(solution)/shard_map/step/pallas_call | solution.py:851
  54.2 1.3 %finish.1 = (f32[8,2,64,128]{3,2,1,0:T(8,128)}, f32[1,64]{1,0:T(1,128)}) custom-call(f32[8,2,64,128]{3,2,1,0:T(8,128)S(1)} %get-tuple-element.6.total_ref, f32[1,64]{1,0:T(1,128)S(1)} %get-tuple-element.7.ev_ref), custom_call_target="tpu_custom_call" | custom-call | tf_op jit(solution)/shard_map/finish/pallas_call | solution.py:906

commit v7 on v6

--- a/solution.py
+++ b/solution.py
@@ -469,7 +469,7 @@
     prior = jnp.sum(jnp.where(diag, jnp.broadcast_to(prior_ref[...], (kh, k)), 0.0), axis=1, keepdims=True)
     psum[...] = jnp.log(prior) - 0.5 * norm
 
-    rows = 8
+    rows = 16
 
     def score_rows(i, top):
         span = pl.ds(pl.multiple_of(i * rows, rows), rows)

time: 55.8 us -> 55.4 us (level)
  no operation moved by 1% of the time
where the time goes in v7:
time: 55.4 us; the launch traced here: 55.2 us
  Pallas kernels  54.4 us (98%)
  between operations  0.8 us (1%)
    pallas_call x1, Pallas kernels, shards(): pl.pallas_call(functools.partial(step_kernel, zn, dp, window), out_shape=...  53.1 us
    pallas_call x1, Pallas kernels, shards(): pl.pallas_call(finish_kernel, out_shape=(jax.ShapeDtypeStruct((mb, 2, kh,...  1.31 us

profile of v7, /device:TPU:0, one launch (start us, length us, event | category | flops | bytes accessed | tf_op | source)
XLA Modules:
  0.0 55.2 jit_solution(18205509483185506188)
XLA Ops:
  0.6 53.1 %step.1 = (f32[8,2,64,128]{3,2,1,0:T(8,128)S(1)}, f32[1,64]{1,0:T(1,128)S(1)}) custom-call(bf16[8,2,64,128]{3,2,1,0:T(8,128)(2,1)} %bitcast.7, bf16[64,128,128]{2,1,0:T(8,128)(2,1)} %refs_1_.1, s32[1,64]{1,0:T(1,128)} %bitcast.8, f32[1,32]{1,0:T(1,128)} %bitcast.9, f32[1,64]{1,0:T(1,128)} %bitcast.10, f32[1,128]{1,0:T(1,128)} %bitcast.11), custom_call_target="tpu_custom_call" | custom-call | tf_op jit(solution)/shard_map/step/pallas_call | solution.py:851
  53.8 1.3 %finish.1 = (f32[8,2,64,128]{3,2,1,0:T(8,128)}, f32[1,64]{1,0:T(1,128)}) custom-call(f32[8,2,64,128]{3,2,1,0:T(8,128)S(1)} %get-tuple-element.6.total_ref, f32[1,64]{1,0:T(1,128)S(1)} %get-tuple-element.7.ev_ref), custom_call_target="tpu_custom_call" | custom-call | tf_op jit(solution)/shard_map/finish/pallas_call | solution.py:906
